TPU v7x, 32 devices: a whole 2x2x4 slice. The times are simulated.
32 devices in a mesh: dp: 8 (over z, x), table: 4 (over y, core).
Axes of the slice: x: 2, y: 2, z: 4, core: 2. Of those that a mesh axis runs over, the one named last changes fastest.
Arguments:
- feature_high: int32 [20, 2048], P(None, 'dp'), may hold values from 0 to 2047
- feature_low: int32 [20, 2048], P(None, 'dp'), may hold values from 0 to 2047
- labels: int32 [2048], P('dp'), may hold values 0 or 1
- weights: float32 [4194304], P(('dp', 'table')), may hold values from -0.6 to 0.6
- history_steps: float32 [8, 4194304], P(None, ('dp', 'table')), may hold values from -46 to 46
- history_diffs: float32 [8, 4194304], P(None, ('dp', 'table')), may hold values from -198 to 198, as said below
Outputs:
- direction: float32 [4194304], P(('dp', 'table'))
Inputs may be any that keep to these rules, and one draw needn't show every extreme that they name: Each entry of history_diffs has the sign of the matching entry of history_steps and 0.2 to 4.3 times its magnitude.
All inputs are finite; a program needn't handle non-finite values. No bound on the sum of `labels` on one device may be relied on, other than what follows from the above.
Results may differ from a plain program's by a relative error of at most 0.0001.
Values sent between devices are 32-bit elements; how exact they have to be, the bound alone decides.
A program may use at most 64 MiB of HBM per device.

v0:
```python
import jax
import jax.numpy as jnp
from jax import lax
from jax.sharding import PartitionSpec as P

TABLE = 4194304
HASHES = 4


high_mult = (40503, 96469, 255361, 362443)
low_mult = (2053, 6151, 12289, 98317)
slot_mult = (1543, 3079, 769, 3457)
shifts = (0, 1048573, 2097143, 3145727)
l2_weight = 1.0


def hashed(feature_high, feature_low, number):
    slot_index = jnp.arange(feature_high.shape[0], dtype=jnp.int32)[:, None]
    part_high = feature_high * high_mult[number] % TABLE
    part_low = feature_low * low_mult[number] % TABLE
    return (part_high + part_low + slot_index * slot_mult[number] + shifts[number]) % TABLE


def local(feature_high, feature_low, labels, weights, history_steps, history_diffs):
    width = weights.shape[0]
    shard_count = lax.axis_size("table")
    column = lax.axis_index("table")
    gathered = lax.all_gather(weights, "dp", axis=0, tiled=True)
    margin = jnp.zeros((feature_high.shape[1],), jnp.float32)
    owned_list = []
    position_list = []
    for number in range(HASHES):
        indices = hashed(feature_high, feature_low, number)
        blocks = indices // width
        owned = blocks % shard_count == column
        position = blocks // shard_count * width + indices % width
        owned_list.append(owned)
        position_list.append(position)
        margin = margin + jnp.sum(jnp.where(owned, gathered[position], 0.0), axis=0)
    margin = lax.psum(margin, "table")
    residual = jax.nn.sigmoid(margin) - labels.astype(jnp.float32)
    all_positions = jnp.concatenate([place.reshape(-1) for place in position_list])
    all_terms = jnp.concatenate(
        [jnp.where(owned, residual[None, :], 0.0).reshape(-1) for owned in owned_list]
    )
    partial_grad = jnp.zeros(gathered.shape, jnp.float32).at[all_positions].add(all_terms)
    summed = lax.psum(partial_grad, "dp")
    mine = lax.dynamic_slice_in_dim(summed, lax.axis_index("dp") * width, width)
    gradient = mine + l2_weight * weights
    memory = history_steps.shape[0]
    newest = memory - 1
    pair_sums, newest_square = lax.psum(
        (
            jnp.sum(history_steps * history_diffs, axis=1),
            jnp.sum(history_diffs[newest] * history_diffs[newest]),
        ),
        ("dp", "table"),
    )
    inverse = 1.0 / pair_sums
    current = gradient
    alphas = [None] * memory
    for which in reversed(range(memory)):
        alphas[which] = inverse[which] * lax.psum(
            jnp.sum(history_steps[which] * current), ("dp", "table")
        )
        current = current - alphas[which] * history_diffs[which]
    current = pair_sums[newest] / newest_square * current
    for which in range(memory):
        correction = inverse[which] * lax.psum(
            jnp.sum(history_diffs[which] * current), ("dp", "table")
        )
        current = current + (alphas[which] - correction) * history_steps[which]
    return -current


def solution(mesh):
    placed = (
        P(None, "dp"),
        P(None, "dp"),
        P("dp"),
        P(("dp", "table")),
        P(None, ("dp", "table")),
        P(None, ("dp", "table")),
    )
    return jax.shard_map(
        local, mesh=mesh, in_specs=placed, out_specs=P(("dp", "table")), check_vma=False
    )
```

profile of v0, /device:TPU:0, one launch (start us, length us, event | category | flops | bytes accessed | tf_op | source)
XLA Modules:
  0.0 1326.4 jit_solution(4070910795745092147)
XLA Ops:
  6.5 0.0 all-gather.2.cloned.1.call-start
  6.5 0.7 all-gather.2.cloned.1.call-update
  7.3 0.0 all-reduce.4.cloned.1.call-start
  7.3 1.1 compare_select_fusion.1
  8.7 0.1 compare_select_fusion
  8.8 76.8 %all-gather.2.cloned.1.call-done = f32[1048576]{0:T(1024)} async-done(((f32[131072]{0:T(1024)}), f32[1048576]{0:T(1024)}) %all-gather.2.cloned.1.call-update) | async-done | bytes 4194320 | tf_op jit(solution)/shard_map/all_gather | solution.py:28
  85.6 60.4 %gather_fusion.3 = f32[5120]{0:T(1024)S(1)} fusion(f32[1048576]{0:T(1024)} %all-gather.2.cloned.1.call-done, s32[5120]{0:T(1024)S(1)} %broadcast_clamp_fusion), kind=kCustom, calls=%fused_computation.3 | custom fusion | bytes 61440 | tf_op jit(solution)/shard_map/gather | solution.py:39
  146.0 60.4 %gather_fusion.1 = f32[5120]{0:T(1024)S(1)} fusion(f32[1048576]{0:T(1024)} %all-gather.2.cloned.1.call-done, s32[5120]{0:T(1024)S(1)} %broadcast_clamp_fusion.2), kind=kCustom, calls=%fused_computation.1 | custom fusion | bytes 61440 | tf_op jit(solution)/shard_map/gather | solution.py:39
  206.5 60.4 %gather_fusion = f32[5120]{0:T(1024)S(1)} fusion(f32[1048576]{0:T(1024)} %all-gather.2.cloned.1.call-done, s32[5120]{0:T(1024)S(1)} %broadcast_clamp_fusion.3), kind=kCustom, calls=%fused_computation | custom fusion | bytes 61440 | tf_op jit(solution)/shard_map/gather | solution.py:39
  266.9 0.0 copy-start.4
  266.9 60.4 %gather_fusion.2 = f32[5120]{0:T(1024)S(1)} fusion(f32[1048576]{0:T(1024)} %all-gather.2.cloned.1.call-done, s32[5120]{0:T(1024)S(1)} %broadcast_clamp_fusion.1), kind=kCustom, calls=%fused_computation.2 | custom fusion | bytes 61440 | tf_op jit(solution)/shard_map/gather | solution.py:39
  327.4 0.1 select_reduce_fusion.2
  327.4 0.1 select_reduce_fusion
  327.5 5.7 psum.142
  333.2 0.0 copy-done.4
  333.3 109.3 %scatter_custom_fusion = f32[1048576]{0:T(1024)} fusion(s32[20480]{0:T(1024)S(1)} %bitcast.84, f32[20480]{0:T(1024)S(1)} %pad_maximum_fusion, f32[]{:T(128)} %constant.207.clone.1), kind=kCustom, calls=%fused_computation.6 | custom fusion | flops 20480 | bytes 4194308 | tf_op jit(solution)/shard_map/scatter-add | solution.py:46
  442.6 0.0 all-reduce.4.cloned.1.call-update
  442.6 16.4 %fusion.62 = (f32[1,131072]{1,0:T(1,128)S(1)}, f32[1,131072]{1,0:T(1,128)}, f32[1,131072]{1,0:T(1,128)S(1)}, f32[1,131072]{1,0:T(1,128)}, f32[1,131072]{1,0:T(1,...) fusion(f32[8,131072]{1,0:T(8,128)} %param.10), kind=kLoop, calls=%fused_computation.207 | loop fusion | bytes 8388608 | tf_op jit(solution)/shard_map/slice | solution.py:64
  459.1 0.0 copy-start
  459.1 0.0 copy-start.3
  459.1 4.8 multiply_reduce_fusion
  463.9 133.8 %all-reduce.4.cloned.1.call-done = f32[1048576]{0:T(1024)} async-done(((f32[1048576]{0:T(1024)}), f32[1048576]{0:T(1024)}) %all-reduce.4.cloned.1.call-update) | async-done | bytes 4194320 | tf_op jit(solution)/shard_map/psum | solution.py:47
  597.7 0.0 copy-done
  597.7 0.0 copy-done.3
  597.7 1.8 multiply_reduce_fusion.16
  599.4 16.6 %fusion.61 = (f32[1,131072]{1,0:T(1,128)}, f32[1,131072]{1,0:T(1,128)S(1)}, f32[1,131072]{1,0:T(1,128)}, f32[1,131072]{1,0:T(1,128)S(1)}, f32[1,131072]{1,0:T(1,...) fusion(f32[8,131072]{1,0:T(8,128)} %param.11), kind=kLoop, calls=%fused_computation.206 | loop fusion | bytes 8388608 | tf_op jit(solution)/shard_map/slice | solution.py:66
  616.0 39.4 %all-reduce.1 = (f32[8]{0:T(128)S(1)}, f32[]{:T(128)}) all-reduce(f32[8]{0:T(128)S(1)} %multiply_reduce_fusion, f32[]{:T(128)} %multiply_reduce_fusion.16), channel_id=1, replica_groups=mesh['dp'=8,'table'=4] {'dp','table'}, use_global_device_ids=true, to_apply=%region_1.2 | all-reduce | flops 9 | bytes 72 | tf_op jit(solution)/shard_map/psum | solution.py:52
  655.4 0.7 fusion.63
  657.3 3.1 multiply_reduce_fusion.15
  660.4 40.3 %psum.145 = f32[]{:T(128)} all-reduce(f32[]{:T(128)} %get-tuple-element.23), channel_id=1, replica_groups=mesh['dp'=8,'table'=4] {'dp','table'}, use_global_device_ids=true, to_apply=%region_14.15 | all-reduce | flops 1 | bytes 8 | tf_op jit(solution)/shard_map/psum | solution.py:63
  701.9 1.9 multiply_reduce_fusion.14
  703.8 40.7 %psum.146 = f32[]{:T(128)} all-reduce(f32[]{:T(128)} %multiply_reduce_fusion.14), channel_id=1, replica_groups=mesh['dp'=8,'table'=4] {'dp','table'}, use_global_device_ids=true, to_apply=%region_16.17 | all-reduce | flops 1 | bytes 8 | tf_op jit(solution)/shard_map/psum | solution.py:63
  745.8 2.9 multiply_reduce_fusion.13
  748.7 40.4 %psum.147 = f32[]{:T(128)} all-reduce(f32[]{:T(128)} %get-tuple-element.21), channel_id=1, replica_groups=mesh['dp'=8,'table'=4] {'dp','table'}, use_global_device_ids=true, to_apply=%region_18.19 | all-reduce | flops 1 | bytes 8 | tf_op jit(solution)/shard_map/psum | solution.py:63
  790.4 1.9 multiply_reduce_fusion.12
  792.3 40.6 %psum.148 = f32[]{:T(128)} all-reduce(f32[]{:T(128)} %multiply_reduce_fusion.12), channel_id=1, replica_groups=mesh['dp'=8,'table'=4] {'dp','table'}, use_global_device_ids=true, to_apply=%region_20.21 | all-reduce | flops 1 | bytes 8 | tf_op jit(solution)/shard_map/psum | solution.py:63
  834.2 3.0 multiply_reduce_fusion.11
  837.2 40.3 %psum.149 = f32[]{:T(128)} all-reduce(f32[]{:T(128)} %get-tuple-element.19), channel_id=1, replica_groups=mesh['dp'=8,'table'=4] {'dp','table'}, use_global_device_ids=true, to_apply=%region_22.23 | all-reduce | flops 1 | bytes 8 | tf_op jit(solution)/shard_map/psum | solution.py:63
  878.8 1.8 multiply_reduce_fusion.10
  880.6 0.7 slice.50
  881.2 40.6 %psum.150 = f32[]{:T(128)} all-reduce(f32[]{:T(128)} %multiply_reduce_fusion.10), channel_id=1, replica_groups=mesh['dp'=8,'table'=4] {'dp','table'}, use_global_device_ids=true, to_apply=%region_24.25 | all-reduce | flops 1 | bytes 8 | tf_op jit(solution)/shard_map/psum | solution.py:63
  923.1 2.9 multiply_reduce_fusion.9
  926.0 40.2 %all-reduce = (f32[]{:T(128)}, f32[]{:T(128)}) all-reduce(f32[]{:T(128)} %get-tuple-element.17, f32[]{:T(128)} %get-tuple-element.61), channel_id=1, replica_groups=mesh['dp'=8,'table'=4] {'dp','table'}, use_global_device_ids=true, to_apply=%region_26.27 | all-reduce | flops 2 | bytes 16 | tf_op jit(solution)/shard_map/psum | solution.py:63
  968.9 1.9 multiply_reduce_fusion.8
  970.8 40.6 %psum.152 = f32[]{:T(128)} all-reduce(f32[]{:T(128)} %multiply_reduce_fusion.8), channel_id=1, replica_groups=mesh['dp'=8,'table'=4] {'dp','table'}, use_global_device_ids=true, to_apply=%region_28.29 | all-reduce | flops 1 | bytes 8 | tf_op jit(solution)/shard_map/psum | solution.py:69
  1012.5 3.1 multiply_reduce_fusion.7
  1015.6 40.1 %psum.153 = f32[]{:T(128)} all-reduce(f32[]{:T(128)} %get-tuple-element.15), channel_id=1, replica_groups=mesh['dp'=8,'table'=4] {'dp','table'}, use_global_device_ids=true, to_apply=%region_30.31 | all-reduce | flops 1 | bytes 8 | tf_op jit(solution)/shard_map/psum | solution.py:69
  1057.0 1.9 multiply_reduce_fusion.6
  1058.8 40.7 %psum.154 = f32[]{:T(128)} all-reduce(f32[]{:T(128)} %multiply_reduce_fusion.6), channel_id=1, replica_groups=mesh['dp'=8,'table'=4] {'dp','table'}, use_global_device_ids=true, to_apply=%region_32.33 | all-reduce | flops 1 | bytes 8 | tf_op jit(solution)/shard_map/psum | solution.py:69
  1100.8 0.0 copy-start.2
  1100.8 2.9 multiply_reduce_fusion.5
  1103.8 40.1 %psum.155 = f32[]{:T(128)} all-reduce(f32[]{:T(128)} %get-tuple-element.13), channel_id=1, replica_groups=mesh['dp'=8,'table'=4] {'dp','table'}, use_global_device_ids=true, to_apply=%region_34.35 | all-reduce | flops 1 | bytes 8 | tf_op jit(solution)/shard_map/psum | solution.py:69
  1145.3 0.0 copy-start.1
  1145.3 1.9 multiply_reduce_fusion.4
  1147.2 40.7 %psum.156 = f32[]{:T(128)} all-reduce(f32[]{:T(128)} %multiply_reduce_fusion.4), channel_id=1, replica_groups=mesh['dp'=8,'table'=4] {'dp','table'}, use_global_device_ids=true, to_apply=%region_36.37 | all-reduce | flops 1 | bytes 8 | tf_op jit(solution)/shard_map/psum | solution.py:69
  1189.3 2.2 multiply_reduce_fusion.3
  1191.5 40.2 %psum.157 = f32[]{:T(128)} all-reduce(f32[]{:T(128)} %get-tuple-element.11), channel_id=1, replica_groups=mesh['dp'=8,'table'=4] {'dp','table'}, use_global_device_ids=true, to_apply=%region_38.39 | all-reduce | flops 1 | bytes 8 | tf_op jit(solution)/shard_map/psum | solution.py:69
  1233.0 0.7 multiply_reduce_fusion.2
  1233.7 40.6 %psum.158 = f32[]{:T(128)} all-reduce(f32[]{:T(128)} %multiply_reduce_fusion.2), channel_id=1, replica_groups=mesh['dp'=8,'table'=4] {'dp','table'}, use_global_device_ids=true, to_apply=%region_40.41 | all-reduce | flops 1 | bytes 8 | tf_op jit(solution)/shard_map/psum | solution.py:69
  1275.5 0.0 copy-done.2
  1275.5 1.8 multiply_reduce_fusion.1
  1277.3 40.1 %psum.159 = f32[]{:T(128)} all-reduce(f32[]{:T(128)} %get-tuple-element.9), channel_id=1, replica_groups=mesh['dp'=8,'table'=4] {'dp','table'}, use_global_device_ids=true, to_apply=%region_42.43 | all-reduce | flops 1 | bytes 8 | tf_op jit(solution)/shard_map/psum | solution.py:69
  1318.7 0.0 copy-done.1
  1318.7 0.8 add_negate_fusion
  (33 shorter events, 0.3 us)
Async XLA Ops:
  6.5 79.1 %all-gather.2.cloned.1.call-start = ((), (), s32[]{:S(2)}) async-start(), calls=%async_computation | async-start | bytes 4718592 | tf_op jit(solution)/shard_map/all_gather | solution.py:28
  7.3 590.4 %all-reduce.4.cloned.1.call-start = ((), (), s32[]{:S(2)}) async-start(), calls=%async_computation.1 | async-start | bytes 8388608 | tf_op jit(solution)/shard_map/psum | solution.py:47
  266.9 66.3 %copy-start.4 = (s32[256]{0:T(256)S(1)}, s32[256]{0:T(256)}, u32[]{:S(2)}) copy-start(s32[256]{0:T(256)} %param.8) | copy-start | bytes 3076
  459.1 138.6 %copy-start = (f32[1,131072]{1,0:T(1,128)}, f32[1,131072]{1,0:T(1,128)S(1)}, u32[]{:S(2)}) copy-start(f32[1,131072]{1,0:T(1,128)S(1)} %get-tuple-element.59) | copy-start | bytes 1572868
  459.1 138.6 %copy-start.3 = (f32[131072]{0:T(1024)S(1)}, f32[131072]{0:T(1024)}, u32[]{:S(2)}) copy-start(f32[131072]{0:T(1024)} %param.9) | copy-start | bytes 1572868
  1100.8 174.7 %copy-start.2 = (f32[1,131072]{1,0:T(1,128)S(1)}, f32[1,131072]{1,0:T(1,128)}, u32[]{:S(2)}) copy-start(f32[1,131072]{1,0:T(1,128)} %get-tuple-element.58) | copy-start | bytes 1572868
  1145.3 173.4 %copy-start.1 = (f32[1,131072]{1,0:T(1,128)S(1)}, f32[1,131072]{1,0:T(1,128)}, u32[]{:S(2)}) copy-start(f32[1,131072]{1,0:T(1,128)} %copy-done) | copy-start | bytes 1572868
Sparse Core Ops, SparseCore 0:
  9.5 76.0 all-gather.1
  442.8 154.8 all-reduce.3
where the time goes:
time: 1340 us; the launch traced here: 1330 us
  blocking collectives  651 us (49%)
  local copies, waits for them, and re-layouts  276 us (21%)
  waiting for transfers between devices  211 us (16%)
  other arithmetic  152 us (11%)
  between operations  35.7 us (3%)
    psum x8, blocking collectives, local(): lax.psum(jnp.sum(history_diffs[which] * current), ('dp', 'table'))  323 us
    psum x7, blocking collectives, local(): lax.psum(jnp.sum(history_steps[which] * current), ('dp', 'table'))  283 us
    gather x8, local copies, waits for them, and re-layouts, local(): margin = margin + jnp.sum(jnp.where(owned, gathered[position], 0.0), axis=0)  242 us
    psum x1, waiting for transfers between devices, local(): summed = lax.psum(partial_grad, 'dp')  134 us
    scatter-add x1, other arithmetic, local(): jnp.zeros(gathered.shape, jnp.float32).at[all_positions].add(all_terms)  109 us
    all_gather x1, waiting for transfers between devices, local(): gathered = lax.all_gather(weights, 'dp', axis=0, tiled=True)  76.8 us
    psum x1, blocking collectives, local(): lax.psum((jnp.sum(history_steps * history_diffs, axis=1), jnp.sum(history...  39.4 us
  transfers between devices with their start and end apart: 2, of which 2 were waited for; matrix products, arithmetic and copies ran while one was open for 2% of the time, Pallas kernels for 0%

commit v1 on v0

v1 whole, which is shorter than its diff:
```python
import functools

import jax
import jax.numpy as jnp
from jax import lax
from jax.experimental import pallas as pl
from jax.experimental.pallas import tpu as pltpu
from jax.sharding import PartitionSpec as P

HASHES = 4
LANES = 128
BLOCK = 16
GROUP = 4

high_mult = (40503, 96469, 255361, 362443)
low_mult = (2053, 6151, 12289, 98317)
slot_mult = (1543, 3079, 769, 3457)
shifts = (0, 1048573, 2097143, 3145727)
l2_weight = 1.0
F32, BF16, I32 = jnp.float32, jnp.bfloat16, jnp.int32


def iota(shape, axis):
    return lax.broadcasted_iota(I32, shape, axis)


def split(value):
    top = value.astype(BF16)
    return top, (value - top.astype(F32)).astype(BF16)


def hot(index, count):
    shape = (count, index.shape[1])
    return jnp.where(iota(shape, 0) == index, 1.0, 0.0).astype(BF16)


def gram_kernel(steps_ref, diffs_ref, out_ref, sums):
    @pl.when(pl.program_id(0) == 0)
    def _():
        sums[...] = jnp.zeros_like(sums)

    mem = steps_ref.shape[0]

    def body(number, carry):
        at = pl.ds(pl.multiple_of(number * LANES, LANES), LANES)
        step, diff = steps_ref[:, at], diffs_ref[:, at]
        new = []
        for i in range(mem):
            row = jnp.broadcast_to(diff[i : i + 1], diff.shape)
            new.append(carry[2 * i] + step * row)
            new.append(carry[2 * i + 1] + diff * row)
        return tuple(new)

    start = tuple(sums[i] for i in range(2 * mem))
    final = lax.fori_loop(0, steps_ref.shape[1] // LANES, body, start, unroll=4)
    for i in range(2 * mem):
        sums[i] = final[i]

    @pl.when(pl.program_id(0) == pl.num_programs(0) - 1)
    def _():
        lane = iota((mem, LANES), 1)
        total = jnp.zeros((mem, LANES), F32)
        for i in range(mem):
            for kind in range(2):
                column = jnp.sum(final[2 * i + kind], axis=1, keepdims=True)
                total = jnp.where(lane == kind * mem + i, column, total)
        out_ref[...] = total


def gram(steps, diffs):
    mem, width = steps.shape
    chunk = min(width, 16384)
    return pl.pallas_call(
        gram_kernel,
        grid=(width // chunk,),
        in_specs=[pl.BlockSpec((mem, chunk), lambda i: (0, i))] * 2,
        out_specs=pl.BlockSpec((mem, LANES), lambda i: (0, 0)),
        out_shape=jax.ShapeDtypeStruct((mem, LANES), F32),
        scratch_shapes=[pltpu.VMEM((2 * mem, mem, LANES), F32)],
        cost_estimate=pl.CostEstimate(flops=32 * mem * width, bytes_accessed=8 * mem * width, transcendentals=0),
        name="gram",
    )(steps, diffs)


def margin_kernel(count, subs, bits, high_ref, low_ref, weights_ref, margin_ref, slots_ref, levels_ref, table):
    device = lax.axis_index("dp") * lax.axis_size("table") + lax.axis_index("table")
    width = 1 << bits
    slot_total = high_ref.shape[0]
    tops, rests = split(weights_ref[...].T)
    table[: LANES] = tops
    table[LANES :] = rests

    def one_pass(number, _):
        base = number * BLOCK

        def body(slot, carry):
            seen, outs = carry[0], list(carry[1:])
            for sub in range(subs):
                group, half = sub // 2, sub % 2
                at = (slot, pl.ds(group * 8, 8), pl.ds(half * LANES, LANES))
                high, low = high_ref[at], low_ref[at]
                for k in range(HASHES):
                    index = (high * high_mult[k] + low * low_mult[k] + (slot * slot_mult[k] + shifts[k])) & (count - 1)
                    owned = (index >> bits) == device
                    place = jnp.where(owned, seen, -1)
                    code = (index & (width - 1)) | (sub << bits)
                    for level in range(BLOCK):
                        outs[level] = jnp.where(place == level, code, outs[level])
                    seen = seen + owned.astype(I32)
            return (seen, *outs)

        empty = jnp.full((8, LANES), -1, I32)
        final = lax.fori_loop(0, slot_total, body, (jnp.zeros((8, LANES), I32) - base,) + (empty,) * BLOCK)
        for level in range(BLOCK):
            slots_ref[:, base + level, :] = final[1 + level]
        return final[0] + base

    seen = one_pass(0, None)
    most = jnp.max(seen)
    lax.fori_loop(1, (most + BLOCK - 1) // BLOCK, lambda n, c: (one_pass(n, None), c)[1], 0)
    for row in range(8):
        levels_ref[row] = (jnp.max(seen[row : row + 1]) + GROUP - 1) // GROUP

    def rows(row, _):
        def body(number, total):
            codes = slots_ref[row, pl.ds(number * GROUP, GROUP), :]
            code = jnp.concatenate([codes[i : i + 1] for i in range(GROUP)], axis=1)
            local = code & (width - 1)
            found = jnp.dot(table[...], hot(local >> 7, width // LANES), preferred_element_type=F32)
            found = found[:LANES] + found[LANES:]
            chosen = jnp.where(iota(found.shape, 0) == (local & (LANES - 1)), found, 0.0)
            value = jnp.sum(chosen, axis=0, keepdims=True)
            sub = code >> bits
            for i in range(GROUP):
                at = slice(i * LANES, (i + 1) * LANES)
                total = total + jnp.where(iota((subs, LANES), 0) == sub[:, at], value[:, at], 0.0)
            return total

        margin_ref[row] = lax.fori_loop(0, levels_ref[row], body, jnp.zeros((subs, LANES), F32))
        return 0

    lax.fori_loop(0, 8, rows, 0)


def margins(high, low, weights, count, subs, bits):
    levels = -(-subs * HASHES * high.shape[0] // BLOCK) * BLOCK
    vmem = pl.BlockSpec(memory_space=pltpu.VMEM)
    return pl.pallas_call(
        functools.partial(margin_kernel, count, subs, bits),
        in_specs=[vmem] * 3,
        out_specs=[vmem, vmem, pl.BlockSpec(memory_space=pltpu.SMEM)],
        out_shape=[
            jax.ShapeDtypeStruct((8, subs, LANES), F32),
            jax.ShapeDtypeStruct((8, levels, LANES), I32),
            jax.ShapeDtypeStruct((8,), I32),
        ],
        scratch_shapes=[pltpu.VMEM((2 * LANES, (1 << bits) // LANES), BF16)],
        compiler_params=pltpu.CompilerParams(vmem_limit_bytes=40 << 20),
        name="margins",
    )(high, low, weights)


def gradient_kernel(subs, bits, margin_ref, labels_ref, slots_ref, levels_ref, weights_ref, steps_hbm, diffs_hbm,
                    gradient_ref, products_ref, residual, both, steps, diffs, sems):
    copies = [
        pltpu.make_async_copy(steps_hbm, steps, sems.at[0]),
        pltpu.make_async_copy(diffs_hbm, diffs, sems.at[1]),
    ]
    for copy in copies:
        copy.start()
    width = 1 << bits
    residual[...] = 1.0 / (1.0 + jnp.exp(-margin_ref[...])) - labels_ref[...].astype(F32)
    both[...] = jnp.zeros_like(both)

    def rows(row, _):
        value = residual[row]

        def body(number, _):
            codes = slots_ref[row, pl.ds(number * GROUP, GROUP), :]
            code = jnp.concatenate([codes[i : i + 1] for i in range(GROUP)], axis=1)
            local = code & (width - 1)
            sub = code >> bits
            wide = jnp.concatenate([value] * GROUP, axis=1)
            mine = jnp.sum(jnp.where(iota(wide.shape, 0) == sub, wide, 0.0), axis=0, keepdims=True)
            column = iota((LANES, GROUP * LANES), 0) == (local & (LANES - 1))
            top, rest = split(jnp.where(column, mine, 0.0))
            terms = jnp.concatenate([top, rest], axis=0)
            both[...] += lax.dot_general(
                hot(local >> 7, width // LANES), terms, (((1,), (1,)), ((), ())), preferred_element_type=F32
            )
            return 0

        lax.fori_loop(0, levels_ref[row], body, 0)
        return 0

    lax.fori_loop(0, 8, rows, 0)
    gradient_ref[...] = both[:, :LANES] + both[:, LANES:] + l2_weight * weights_ref[...]
    for copy in copies:
        copy.wait()
    mem = steps.shape[0]

    def body(number, carry):
        by_step, by_diff = carry
        tile = gradient_ref[pl.ds(pl.multiple_of(number * 8, 8), 8), :]
        for i in range(8):
            at = pl.ds(pl.multiple_of(number * 8 * LANES, LANES) + i * LANES, LANES)
            row = jnp.broadcast_to(tile[i : i + 1], (mem, LANES))
            by_step = by_step + steps[:, at] * row
            by_diff = by_diff + diffs[:, at] * row
        return by_step, by_diff

    zero = jnp.zeros((mem, LANES), F32)
    by_step, by_diff = lax.fori_loop(0, width // (8 * LANES), body, (zero, zero))
    lane = iota((mem, LANES), 1)
    products_ref[...] = jnp.where(
        lane == 0,
        jnp.sum(by_step, axis=1, keepdims=True),
        jnp.where(lane == 1, jnp.sum(by_diff, axis=1, keepdims=True), 0.0),
    )


def gradients(margin, labels, slots, levels, weights, steps, diffs, subs, bits):
    vmem = pl.BlockSpec(memory_space=pltpu.VMEM)
    hbm = pl.BlockSpec(memory_space=pl.ANY)
    mem, width = steps.shape
    return pl.pallas_call(
        functools.partial(gradient_kernel, subs, bits),
        in_specs=[vmem, vmem, vmem, pl.BlockSpec(memory_space=pltpu.SMEM), vmem, hbm, hbm],
        out_specs=[vmem, vmem],
        out_shape=[jax.ShapeDtypeStruct(weights.shape, F32), jax.ShapeDtypeStruct((mem, LANES), F32)],
        scratch_shapes=[
            pltpu.VMEM(margin.shape, F32),
            pltpu.VMEM((width // LANES, 2 * LANES), F32),
            pltpu.VMEM((mem, width), F32),
            pltpu.VMEM((mem, width), F32),
            pltpu.SemaphoreType.DMA((2,)),
        ],
        compiler_params=pltpu.CompilerParams(vmem_limit_bytes=40 << 20),
        name="gradient",
    )(margin, labels, slots, levels, weights, steps, diffs)


def coefficients(grams, products, mem):
    lane, place = iota((mem, LANES), 1), iota((mem, LANES), 0)

    def column(array, number):
        return jnp.broadcast_to(
            jnp.sum(jnp.where(lane == number, array, 0.0), axis=1, keepdims=True), (mem, LANES)
        )

    def pick(array, number):
        return jnp.broadcast_to(array[number : number + 1], (mem, LANES))

    cross = [column(grams, i) for i in range(mem)]
    square = [column(grams, mem + i) for i in range(mem)]
    pairs = [pick(cross[i], i) for i in range(mem)]
    inverse = [1.0 / pair for pair in pairs]
    by_step, by_diff = column(products, 0), column(products, 1)
    alphas = [None] * mem
    for i in reversed(range(mem)):
        alphas[i] = inverse[i] * pick(by_step, i)
        by_step = by_step - alphas[i] * cross[i]
        by_diff = by_diff - alphas[i] * square[i]
    scale = pairs[mem - 1] / pick(square[mem - 1], mem - 1)
    by_diff = scale * by_diff
    on_steps = jnp.zeros((mem, LANES), F32)
    on_diffs = jnp.zeros((mem, LANES), F32)
    for i in range(mem):
        extra = jnp.sum(on_steps * cross[i], axis=0, keepdims=True)
        beta = inverse[i] * (pick(by_diff, i) + extra)
        on_steps = jnp.where(place == i, alphas[i] - beta, on_steps)
        on_diffs = jnp.where(place == i, -scale * alphas[i], on_diffs)
    return scale, on_diffs, on_steps


def direction_kernel(grams_ref, products_ref, gradient_ref, steps_ref, diffs_ref, out_ref, factors):
    mem = steps_ref.shape[0]

    @pl.when(pl.program_id(0) == 0)
    def _():
        scale, on_diffs, on_steps = coefficients(grams_ref[...], products_ref[...], mem)
        factors[0], factors[1], factors[2] = -scale, -on_diffs, -on_steps

    scale, on_diffs, on_steps = factors[0], factors[1], factors[2]

    def body(number, _):
        rows = []
        for i in range(8):
            at = pl.ds(pl.multiple_of(number * 8 * LANES, LANES) + i * LANES, LANES)
            rows.append(jnp.sum(on_diffs * diffs_ref[:, at] + on_steps * steps_ref[:, at], axis=0, keepdims=True))
        at = pl.ds(pl.multiple_of(number * 8, 8), 8)
        out_ref[at, :] = scale * gradient_ref[at, :] + jnp.concatenate(rows, axis=0)
        return 0

    lax.fori_loop(0, out_ref.shape[0] // 8, body, 0, unroll=2)


def directions(grams, products, gradient, steps, diffs):
    mem, width = steps.shape
    chunk = min(width, 16384)
    whole = pl.BlockSpec((mem, LANES), lambda i: (0, 0))
    flat = pl.BlockSpec((chunk // LANES, LANES), lambda i: (i, 0))
    wide = pl.BlockSpec((mem, chunk), lambda i: (0, i))
    return pl.pallas_call(
        direction_kernel,
        grid=(width // chunk,),
        in_specs=[whole, whole, flat, wide, wide],
        out_specs=flat,
        out_shape=jax.ShapeDtypeStruct(gradient.shape, F32),
        scratch_shapes=[pltpu.VMEM((3, mem, LANES), F32)],
        name="direction",
    )(grams, products, gradient, steps, diffs)


def local(feature_high, feature_low, labels, weights, history_steps, history_diffs):
    width = weights.shape[0]
    parts = lax.axis_size("dp")
    count = width * parts * lax.axis_size("table")
    bits = width.bit_length() - 1
    slots = feature_high.shape[0]
    subs = parts * feature_high.shape[1] // 1024
    mine = jnp.concatenate([feature_high, feature_low, labels[None, :]], axis=0)
    every = lax.all_gather(mine, "dp", axis=1)
    high, low = every[:slots], every[slots : 2 * slots]
    label = every[2 * slots].reshape(parts // 8, 8, 2, LANES).transpose(1, 0, 2, 3).reshape(8, subs, LANES)
    table = weights.reshape(width // LANES, LANES)
    partial_gram = gram(history_steps, history_diffs)
    margin, listed, levels = margins(high, low, table, count, subs, bits)
    margin, grams = lax.psum((margin, partial_gram), ("dp", "table"))
    gradient, products = gradients(
        margin, label, listed, levels, table, history_steps, history_diffs, subs, bits
    )
    products = lax.psum(products, ("dp", "table"))
    return directions(grams, products, gradient, history_steps, history_diffs).reshape(-1)


def solution(mesh):
    placed = (
        P(None, "dp"),
        P(None, "dp"),
        P("dp"),
        P(("dp", "table")),
        P(None, ("dp", "table")),
        P(None, ("dp", "table")),
    )
    return jax.shard_map(
        local, mesh=mesh, in_specs=placed, out_specs=P(("dp", "table")), check_vma=False
    )
```

time: 1340 us -> 170 us (0.13)
  blocking collectives: 651 us -> 113 us
  local copies, waits for them, and re-layouts: 276 us -> 5.37 us
  waiting for transfers between devices: 211 us -> 0 us
  other arithmetic: 152 us -> 0.01 us
  Pallas kernels: 0 us -> 50.4 us
  between operations: 35.7 us -> 0.09 us
    psum x17 -> x2, blocking collectives: 651 us -> 80.6 us  [local(): margin, grams = lax.psum((margin, partial_gram), ('dp', 'table'))]
    gather x8 -> x0, local copies, waits for them, and re-layouts: 242 us -> none  [local(): margin = margin + jnp.sum(jnp.where(owned, gathered[position], 0.0), axis=0)]
    psum x1 -> x0, waiting for transfers between devices: 134 us -> none  [local(): summed = lax.psum(partial_grad, 'dp')]
    scatter-add x1 -> x0, other arithmetic: 109 us -> none  [local(): jnp.zeros(gathered.shape, jnp.float32).at[all_positions].add(all_terms)]
    all_gather x1 -> x0, waiting for transfers between devices: 76.8 us -> none  [local(): gathered = lax.all_gather(weights, 'dp', axis=0, tiled=True)]
    pallas_call x0 -> x4, Pallas kernels: none -> 50.4 us  [the longest x1 17.6 us: gradients(): pl.pallas_call(functools.partial(gradient_kernel, subs, bits), in_specs=[...]
    reduce_sum x19 -> x0, other arithmetic: 40.6 us -> none  [the longest x8 19.2 us: local(): jnp.sum(history_steps[which] * current)]
    slice x4, local copies, waits for them, and re-layouts: 34.3 us -> 0.06 us  [the longest x3 0.05 us: local(): high, low = (every[:slots], every[slots:2 * slots])]
  transfers between devices with their start and end apart: 2 -> 0, of which waited for: 2 -> 0; matrix products, arithmetic and copies ran while one was open for 2% -> 0% of each run, Pallas kernels for 0% -> 0%
where the time goes in v1:
time: 170 us; the launch traced here: 169 us
  blocking collectives  113 us (66%)
  Pallas kernels  50.4 us (30%)
  local copies, waits for them, and re-layouts  5.37 us (3%)
    psum x2, blocking collectives, local(): margin, grams = lax.psum((margin, partial_gram), ('dp', 'table'))  80.6 us
    all_gather x1, blocking collectives, local(): every = lax.all_gather(mine, 'dp', axis=1)  32.8 us
    pallas_call x1, Pallas kernels, gradients(): pl.pallas_call(functools.partial(gradient_kernel, subs, bits), in_specs=[...  17.6 us
    pallas_call x1, Pallas kernels, margins(): pl.pallas_call(functools.partial(margin_kernel, count, subs, bits), in_sp...  15.3 us
    pallas_call x1, Pallas kernels, gram(): pl.pallas_call(gram_kernel, grid=(width // chunk,), in_specs=[pl.BlockSpe...  9.56 us
    pallas_call x1, Pallas kernels, directions(): pl.pallas_call(direction_kernel, grid=(width // chunk,), in_specs=[whole,...  7.87 us
    unnamed x18, local copies, waits for them, and re-layouts  5.31 us

profile of v1, /device:TPU:0, one launch (start us, length us, event | category | flops | bytes accessed | tf_op | source)
XLA Modules:
  0.0 169.2 jit_solution(15190643050877103401)
XLA Ops:
  0.0 0.0 copy-start.4
  0.0 0.0 copy-start.5
  0.0 0.0 copy-start.7
  0.0 0.0 copy-start.2
  0.0 9.6 %gram.1 = f32[8,128]{1,0:T(8,128)} custom-call(f32[8,131072]{1,0:T(8,128)} %steps_ref.3, f32[8,131072]{1,0:T(8,128)} %diffs_ref.3), custom_call_target="tpu_custom_call" | custom-call | flops 33554432 | bytes 8388608 | tf_op jit(solution)/shard_map/gram/pallas_call | solution.py:73
  9.6 0.0 copy-done.4
  9.6 0.0 copy-done.5
  9.6 0.0 copy-done.7
  9.6 32.8 %all-gather = s32[41,2048]{1,0:T(8,128)S(1)} all-gather(s32[41,256]{1,0:T(8,128)S(1)} %pad_add_fusion), channel_id=2, replica_groups=mesh['dp'=8,'table'=4] {'dp'}, dimensions={1}, use_global_device_ids=true | all-gather | bytes 377856 | tf_op jit(solution)/shard_map/all_gather | solution.py:323
  42.4 0.1 copy.8
  42.5 0.1 copy.7
  42.6 0.0 copy-done.2
  42.6 15.3 %margins.1 = (f32[8,2,128]{2,1,0:T(2,128)S(1)}, s32[8,160,128]{2,1,0:T(8,128)S(1)}, s32[8]{0:T(128)S(1)}) custom-call(s32[20,8,256]{2,1,0:T(8,128)S(1)} %slice.18.high_ref, s32[20,8,256]{2,1,0:T(8,128)S(1)} %slice.19.low_ref, f32[1024,128]{1,0:T(8,128)S(1)} %bitcast.10), custom_call_target="tpu_custom_call" | custom-call | tf_op jit(solution)/shard_map/margins/pallas_call | solution.py:148
  58.0 40.2 %psum.22.margin_ref = f32[8,2,128]{2,1,0:T(2,128)S(1)} all-reduce(f32[8,2,128]{2,1,0:T(2,128)S(1)} %get-tuple-element.10), channel_id=1, replica_groups=mesh['dp'=8,'table'=4] {'dp','table'}, use_global_device_ids=true, to_apply=%region_1.0 | all-reduce | flops 2048 | bytes 16384 | tf_op jit(solution)/shard_map/psum | solution.py:329
  98.2 0.0 copy-start
  98.2 2.2 %copy-done = f32[8,131072]{1,0:T(8,128)S(1)} copy-done((f32[8,131072]{1,0:T(8,128)S(1)}, f32[8,131072]{1,0:T(8,128)}, u32[]{:S(2)}) %copy-start) | copy-done | bytes 4194328
  100.4 0.0 copy-start.1
  100.4 2.2 %copy-done.1 = f32[8,131072]{1,0:T(8,128)S(1)} copy-done((f32[8,131072]{1,0:T(8,128)S(1)}, f32[8,131072]{1,0:T(8,128)}, u32[]{:S(2)}) %copy-start.1) | copy-done | bytes 4194328
  102.6 0.0 copy-start.6
  102.6 17.6 %gradient.1 = (f32[1024,128]{1,0:T(8,128)S(1)}, f32[8,128]{1,0:T(8,128)S(1)}) custom-call(f32[8,2,128]{2,1,0:T(2,128)S(1)} %psum.22.margin_ref, s32[8,2,128]{2,1,0:T(2,128)S(1)} %bitcast.12, s32[8,160,128]{2,1,0:T(8,128)S(1)} %get-tuple-element.11.slots_ref, s32[8]{0:T(128)S(1)} %get-tuple-element.12.levels_ref, f32[1024,128]{1,0:T(8,128)S(1)} %bitcast.11, ...), custom_call_target="tpu_custom_call" | custom-call | tf_op jit(solution)/shard_map/gradient/pallas_call | solution.py:226
  120.2 0.0 copy-start.3
  120.2 0.8 copy-done.3
  121.0 0.0 copy-done.6
  121.0 40.3 %all-reduce = (f32[8,128]{1,0:T(8,128)}, f32[8,128]{1,0:T(8,128)}) all-reduce(f32[8,128]{1,0:T(8,128)S(1)} %copy-done.6, f32[8,128]{1,0:T(8,128)S(1)} %get-tuple-element.13), channel_id=1, replica_groups=mesh['dp'=8,'table'=4] {'dp','table'}, use_global_device_ids=true, to_apply=%region_0.0 | all-reduce | flops 2048 | bytes 16384 | tf_op jit(solution)/shard_map/psum | solution.py:329
  161.4 7.9 %direction.1 = f32[1024,128]{1,0:T(8,128)} custom-call(f32[8,128]{1,0:T(8,128)} %get-tuple-element.15.grams_ref, f32[8,128]{1,0:T(8,128)} %get-tuple-element.16.products_ref, f32[1024,128]{1,0:T(8,128)} %copy-done.3, f32[8,131072]{1,0:T(8,128)} %steps_ref.3, f32[8,131072]{1,0:T(8,128)} %diffs_ref.3), custom_call_target="tpu_custom_call" | custom-call | tf_op jit(solution)/shard_map/direction/pallas_call | solution.py:304
  (5 shorter events, 0.1 us)
Async XLA Ops:
  0.0 9.6 %copy-start.4 = (s32[20,256]{1,0:T(8,128)S(1)}, s32[20,256]{1,0:T(8,128)}, u32[]{:S(2)}) copy-start(s32[20,256]{1,0:T(8,128)} %param.7) | copy-start | bytes 61444
  0.0 9.6 %copy-start.5 = (s32[20,256]{1,0:T(8,128)S(1)}, s32[20,256]{1,0:T(8,128)}, u32[]{:S(2)}) copy-start(s32[20,256]{1,0:T(8,128)} %param.6) | copy-start | bytes 61444
  0.0 9.6 %copy-start.7 = (s32[256]{0:T(256)S(1)}, s32[256]{0:T(256)}, u32[]{:S(2)}) copy-start(s32[256]{0:T(256)} %param.8) | copy-start | bytes 3076
  0.0 42.6 %copy-start.2 = (f32[131072]{0:T(1024)S(1)}, f32[131072]{0:T(1024)}, u32[]{:S(2)}) copy-start(f32[131072]{0:T(1024)} %param.9) | copy-start | bytes 1572868
  98.2 2.2 %copy-start = (f32[8,131072]{1,0:T(8,128)S(1)}, f32[8,131072]{1,0:T(8,128)}, u32[]{:S(2)}) copy-start(f32[8,131072]{1,0:T(8,128)} %steps_ref.3) | copy-start | bytes 12582916
  100.4 2.2 %copy-start.1 = (f32[8,131072]{1,0:T(8,128)S(1)}, f32[8,131072]{1,0:T(8,128)}, u32[]{:S(2)}) copy-start(f32[8,131072]{1,0:T(8,128)} %diffs_ref.3) | copy-start | bytes 12582916
  102.6 18.4 %copy-start.6 = (f32[8,128]{1,0:T(8,128)S(1)}, f32[8,128]{1,0:T(8,128)}, u32[]{:S(2)}) copy-start(f32[8,128]{1,0:T(8,128)} %gram.1) | copy-start | bytes 12292
  120.2 0.8 copy-start.3

commit v2 on v1

--- a/solution.py
+++ b/solution.py
@@ -18,6 +18,10 @@
 shifts = (0, 1048573, 2097143, 3145727)
 l2_weight = 1.0
 F32, BF16, I32 = jnp.float32, jnp.bfloat16, jnp.int32
+MESH = pl.DeviceIdType.MESH
+VMEM = pl.BlockSpec(memory_space=pltpu.VMEM)
+HBM = pl.BlockSpec(memory_space=pltpu.HBM)
+SMEM = pl.BlockSpec(memory_space=pltpu.SMEM)
 
 
 def iota(shape, axis):
@@ -34,16 +38,85 @@
     return jnp.where(iota(shape, 0) == index, 1.0, 0.0).astype(BF16)
 
 
-def gram_kernel(steps_ref, diffs_ref, out_ref, sums):
-    @pl.when(pl.program_id(0) == 0)
-    def _():
-        sums[...] = jnp.zeros_like(sums)
-
-    mem = steps_ref.shape[0]
+def greet(peers):
+    barrier = pltpu.get_barrier_semaphore()
+    for peer in peers:
+        pl.semaphore_signal(barrier, inc=1, device_id=peer, device_id_type=MESH)
+    pl.semaphore_wait(barrier, len(peers))
+
+
+def others(axis):
+    size, me = lax.axis_size(axis), lax.axis_index(axis)
+    return [{axis: lax.rem(me + step, size)} for step in range(1, size)]
+
+
+def send(source, target, peers, send_sems, recv_sems):
+    copies = []
+    for number, peer in enumerate(peers):
+        copy = pltpu.make_async_remote_copy(
+            src_ref=source,
+            dst_ref=target,
+            send_sem=send_sems.at[number],
+            recv_sem=recv_sems.at[number],
+            device_id=peer,
+            device_id_type=MESH,
+        )
+        copy.start()
+        copies.append(copy)
+    return copies
+
+
+def all_sum(mine, near, far, near_sems, far_sems):
+    total = mine
+    for axis, held, sems in (("table", near, near_sems), ("dp", far, far_sems)):
+        me = lax.axis_index(axis)
+        held[me] = total
+        for copy in send(held.at[me], held.at[me], others(axis), *sems):
+            copy.wait()
+        total = held[0]
+        for number in range(1, held.shape[0]):
+            total = total + held[number]
+    return total
+
+
+def sum_scratch(shape):
+    near, far = lax.axis_size("table"), lax.axis_size("dp")
+    return [
+        pltpu.VMEM((near, *shape), F32),
+        pltpu.VMEM((far, *shape), F32),
+        pltpu.SemaphoreType.DMA((near - 1,)),
+        pltpu.SemaphoreType.DMA((near - 1,)),
+        pltpu.SemaphoreType.DMA((far - 1,)),
+        pltpu.SemaphoreType.DMA((far - 1,)),
+    ]
+
+
+def share_kernel(high_ref, low_ref, labels_ref, steps_hbm, diffs_hbm, every_ref, gram_ref,
+                 steps, diffs, send_sems, recv_sems, step_sems, diff_sems):
+    mem, width = steps.shape
+    slots = high_ref.shape[0]
+    parts = step_sems.shape[0]
+    copies = []
+    for part in range(parts):
+        at = (slice(None), pl.ds(part * (width // parts), width // parts))
+        for source, target, sems in ((steps_hbm, steps, step_sems), (diffs_hbm, diffs, diff_sems)):
+            copy = pltpu.make_async_copy(source.at[at], target.at[at], sems.at[part])
+            copy.start()
+            copies.append(copy)
+    me = lax.axis_index("dp")
+    every_ref[me, :slots] = high_ref[...]
+    every_ref[me, slots : 2 * slots] = low_ref[...]
+    every_ref[me, 2 * slots : 2 * slots + 1] = labels_ref[...]
+    if every_ref.shape[1] > 2 * slots + 1:
+        rest = every_ref.shape[1] - 2 * slots - 1
+        every_ref[me, 2 * slots + 1 :] = jnp.zeros((rest, labels_ref.shape[1]), I32)
+    peers = others("dp")
+    greet(peers)
+    sent = send(every_ref.at[me], every_ref.at[me], peers, send_sems, recv_sems)
 
     def body(number, carry):
         at = pl.ds(pl.multiple_of(number * LANES, LANES), LANES)
-        step, diff = steps_ref[:, at], diffs_ref[:, at]
+        step, diff = steps[:, at], diffs[:, at]
         new = []
         for i in range(mem):
             row = jnp.broadcast_to(diff[i : i + 1], diff.shape)
@@ -51,41 +124,77 @@
             new.append(carry[2 * i + 1] + diff * row)
         return tuple(new)
 
-    start = tuple(sums[i] for i in range(2 * mem))
-    final = lax.fori_loop(0, steps_ref.shape[1] // LANES, body, start, unroll=4)
-    for i in range(2 * mem):
-        sums[i] = final[i]
-
-    @pl.when(pl.program_id(0) == pl.num_programs(0) - 1)
-    def _():
-        lane = iota((mem, LANES), 1)
-        total = jnp.zeros((mem, LANES), F32)
-        for i in range(mem):
-            for kind in range(2):
-                column = jnp.sum(final[2 * i + kind], axis=1, keepdims=True)
-                total = jnp.where(lane == kind * mem + i, column, total)
-        out_ref[...] = total
-
-
-def gram(steps, diffs):
+    final = (jnp.zeros((mem, LANES), F32),) * (2 * mem)
+    each = width // parts // LANES
+    for part in range(parts):
+        copies[2 * part].wait()
+        copies[2 * part + 1].wait()
+        final = lax.fori_loop(part * each, (part + 1) * each, body, final, unroll=4)
+    lane = iota((mem, LANES), 1)
+    total = jnp.zeros((mem, LANES), F32)
+    for i in range(mem):
+        for kind in range(2):
+            column = jnp.sum(final[2 * i + kind], axis=1, keepdims=True)
+            total = jnp.where(lane == kind * mem + i, column, total)
+    gram_ref[...] = total
+    for copy in sent:
+        copy.wait()
+
+
+def share(high, low, labels, steps, diffs):
     mem, width = steps.shape
-    chunk = min(width, 16384)
+    rows = -(-(2 * high.shape[0] + 1) // 8) * 8
+    dp = lax.axis_size("dp")
+    parts = 4
     return pl.pallas_call(
-        gram_kernel,
-        grid=(width // chunk,),
-        in_specs=[pl.BlockSpec((mem, chunk), lambda i: (0, i))] * 2,
-        out_specs=pl.BlockSpec((mem, LANES), lambda i: (0, 0)),
-        out_shape=jax.ShapeDtypeStruct((mem, LANES), F32),
-        scratch_shapes=[pltpu.VMEM((2 * mem, mem, LANES), F32)],
-        cost_estimate=pl.CostEstimate(flops=32 * mem * width, bytes_accessed=8 * mem * width, transcendentals=0),
-        name="gram",
-    )(steps, diffs)
-
-
-def margin_kernel(count, subs, bits, high_ref, low_ref, weights_ref, margin_ref, slots_ref, levels_ref, table):
+        share_kernel,
+        in_specs=[VMEM] * 3 + [HBM] * 2,
+        out_specs=[VMEM] * 2,
+        out_shape=[
+            jax.ShapeDtypeStruct((dp, rows, high.shape[1]), I32),
+            jax.ShapeDtypeStruct((mem, LANES), F32),
+        ],
+        scratch_shapes=[
+            pltpu.VMEM((mem, width), F32),
+            pltpu.VMEM((mem, width), F32),
+            pltpu.SemaphoreType.DMA((dp - 1,)),
+            pltpu.SemaphoreType.DMA((dp - 1,)),
+            pltpu.SemaphoreType.DMA((parts,)),
+            pltpu.SemaphoreType.DMA((parts,)),
+        ],
+        compiler_params=pltpu.CompilerParams(
+            vmem_limit_bytes=40 << 20, collective_id=0, has_side_effects=True
+        ),
+        name="share",
+    )(high, low, labels.reshape(1, -1), steps, diffs)
+
+
+def reduce_kernel(margin_ref, gram_ref, out_ref, own, near, far, *sems):
+    subs = margin_ref.shape[0]
+    greet(others("table") + others("dp"))
+    own[:subs] = margin_ref[...]
+    own[subs] = gram_ref[...]
+    out_ref[...] = all_sum(own[...], near, far, sems[:2], sems[2:])
+
+
+def reduced(margin, grams):
+    shape = (margin.shape[0] + 1, *margin.shape[1:])
+    return pl.pallas_call(
+        reduce_kernel,
+        in_specs=[VMEM] * 2,
+        out_specs=VMEM,
+        out_shape=jax.ShapeDtypeStruct(shape, F32),
+        scratch_shapes=[pltpu.VMEM(shape, F32)] + sum_scratch(shape),
+        compiler_params=pltpu.CompilerParams(collective_id=1, has_side_effects=True),
+        name="reduce",
+    )(margin, grams)
+
+
+def margin_kernel(count, subs, bits, slot_total, every_ref, weights_ref, margin_ref, slots_ref, levels_ref, table, features):
     device = lax.axis_index("dp") * lax.axis_size("table") + lax.axis_index("table")
     width = 1 << bits
-    slot_total = high_ref.shape[0]
+    for number in range(2 * slot_total):
+        features[number] = every_ref[:, number, :]
     tops, rests = split(weights_ref[...].T)
     table[: LANES] = tops
     table[LANES :] = rests
@@ -97,8 +206,8 @@
             seen, outs = carry[0], list(carry[1:])
             for sub in range(subs):
                 group, half = sub // 2, sub % 2
-                at = (slot, pl.ds(group * 8, 8), pl.ds(half * LANES, LANES))
-                high, low = high_ref[at], low_ref[at]
+                at = (pl.ds(group * 8, 8), pl.ds(half * LANES, LANES))
+                high, low = features[(slot, *at)], features[(slot + slot_total, *at)]
                 for k in range(HASHES):
                     index = (high * high_mult[k] + low * low_mult[k] + (slot * slot_mult[k] + shifts[k])) & (count - 1)
                     owned = (index >> bits) == device
@@ -136,31 +245,37 @@
                 total = total + jnp.where(iota((subs, LANES), 0) == sub[:, at], value[:, at], 0.0)
             return total
 
-        margin_ref[row] = lax.fori_loop(0, levels_ref[row], body, jnp.zeros((subs, LANES), F32))
+        total = lax.fori_loop(0, levels_ref[row], body, jnp.zeros((subs, LANES), F32))
+        for sub in range(subs):
+            here = iota((8, LANES), 0) == row
+            margin_ref[sub] = jnp.where(here, total[sub : sub + 1], margin_ref[sub])
         return 0
 
+    margin_ref[...] = jnp.zeros_like(margin_ref)
     lax.fori_loop(0, 8, rows, 0)
 
 
-def margins(high, low, weights, count, subs, bits):
-    levels = -(-subs * HASHES * high.shape[0] // BLOCK) * BLOCK
-    vmem = pl.BlockSpec(memory_space=pltpu.VMEM)
+def margins(every, weights, count, subs, bits, slots):
+    levels = -(-subs * HASHES * slots // BLOCK) * BLOCK
     return pl.pallas_call(
-        functools.partial(margin_kernel, count, subs, bits),
-        in_specs=[vmem] * 3,
-        out_specs=[vmem, vmem, pl.BlockSpec(memory_space=pltpu.SMEM)],
+        functools.partial(margin_kernel, count, subs, bits, slots),
+        in_specs=[VMEM] * 2,
+        out_specs=[VMEM, VMEM, SMEM],
         out_shape=[
-            jax.ShapeDtypeStruct((8, subs, LANES), F32),
+            jax.ShapeDtypeStruct((subs, 8, LANES), F32),
             jax.ShapeDtypeStruct((8, levels, LANES), I32),
             jax.ShapeDtypeStruct((8,), I32),
         ],
-        scratch_shapes=[pltpu.VMEM((2 * LANES, (1 << bits) // LANES), BF16)],
+        scratch_shapes=[
+            pltpu.VMEM((2 * LANES, (1 << bits) // LANES), BF16),
+            pltpu.VMEM((2 * slots, every.shape[0], every.shape[2]), I32),
+        ],
         compiler_params=pltpu.CompilerParams(vmem_limit_bytes=40 << 20),
         name="margins",
-    )(high, low, weights)
-
-
-def gradient_kernel(subs, bits, margin_ref, labels_ref, slots_ref, levels_ref, weights_ref, steps_hbm, diffs_hbm,
+    )(every, weights)
+
+
+def gradient_kernel(subs, bits, label_row, total_ref, every_ref, slots_ref, levels_ref, weights_ref, steps_hbm, diffs_hbm,
                     gradient_ref, products_ref, residual, both, steps, diffs, sems):
     copies = [
         pltpu.make_async_copy(steps_hbm, steps, sems.at[0]),
@@ -169,7 +284,9 @@
     for copy in copies:
         copy.start()
     width = 1 << bits
-    residual[...] = 1.0 / (1.0 + jnp.exp(-margin_ref[...])) - labels_ref[...].astype(F32)
+    for sub in range(subs):
+        label = every_ref[sub // 2 * 8 : sub // 2 * 8 + 8, label_row, sub % 2 * LANES : sub % 2 * LANES + LANES]
+        residual[:, sub, :] = 1.0 / (1.0 + jnp.exp(-total_ref[sub])) - label.astype(F32)
     both[...] = jnp.zeros_like(both)
 
     def rows(row, _):
@@ -219,17 +336,15 @@
     )
 
 
-def gradients(margin, labels, slots, levels, weights, steps, diffs, subs, bits):
-    vmem = pl.BlockSpec(memory_space=pltpu.VMEM)
-    hbm = pl.BlockSpec(memory_space=pl.ANY)
+def gradients(total, every, slots, levels, weights, steps, diffs, subs, bits, label_row):
     mem, width = steps.shape
     return pl.pallas_call(
-        functools.partial(gradient_kernel, subs, bits),
-        in_specs=[vmem, vmem, vmem, pl.BlockSpec(memory_space=pltpu.SMEM), vmem, hbm, hbm],
-        out_specs=[vmem, vmem],
+        functools.partial(gradient_kernel, subs, bits, label_row),
+        in_specs=[VMEM, VMEM, VMEM, SMEM, VMEM, HBM, HBM],
+        out_specs=[VMEM, VMEM],
         out_shape=[jax.ShapeDtypeStruct(weights.shape, F32), jax.ShapeDtypeStruct((mem, LANES), F32)],
         scratch_shapes=[
-            pltpu.VMEM(margin.shape, F32),
+            pltpu.VMEM((8, subs, LANES), F32),
             pltpu.VMEM((width // LANES, 2 * LANES), F32),
             pltpu.VMEM((mem, width), F32),
             pltpu.VMEM((mem, width), F32),
@@ -237,7 +352,7 @@
         ],
         compiler_params=pltpu.CompilerParams(vmem_limit_bytes=40 << 20),
         name="gradient",
-    )(margin, labels, slots, levels, weights, steps, diffs)
+    )(total, every, slots, levels, weights, steps, diffs)
 
 
 def coefficients(grams, products, mem):
@@ -273,21 +388,27 @@
     return scale, on_diffs, on_steps
 
 
-def direction_kernel(grams_ref, products_ref, gradient_ref, steps_ref, diffs_ref, out_ref, factors):
-    mem = steps_ref.shape[0]
-
-    @pl.when(pl.program_id(0) == 0)
-    def _():
-        scale, on_diffs, on_steps = coefficients(grams_ref[...], products_ref[...], mem)
-        factors[0], factors[1], factors[2] = -scale, -on_diffs, -on_steps
-
-    scale, on_diffs, on_steps = factors[0], factors[1], factors[2]
+def direction_kernel(total_ref, products_ref, gradient_ref, steps_hbm, diffs_hbm, out_ref,
+                     steps, diffs, local_sems, near, far, *sems):
+    mem = steps.shape[0]
+    copies = [
+        pltpu.make_async_copy(steps_hbm, steps, local_sems.at[0]),
+        pltpu.make_async_copy(diffs_hbm, diffs, local_sems.at[1]),
+    ]
+    for copy in copies:
+        copy.start()
+    greet(others("table") + others("dp"))
+    products = all_sum(products_ref[...], near, far, sems[:2], sems[2:])
+    scale, on_diffs, on_steps = coefficients(total_ref[total_ref.shape[0] - 1], products, mem)
+    scale, on_diffs, on_steps = -scale, -on_diffs, -on_steps
+    for copy in copies:
+        copy.wait()
 
     def body(number, _):
         rows = []
         for i in range(8):
             at = pl.ds(pl.multiple_of(number * 8 * LANES, LANES) + i * LANES, LANES)
-            rows.append(jnp.sum(on_diffs * diffs_ref[:, at] + on_steps * steps_ref[:, at], axis=0, keepdims=True))
+            rows.append(jnp.sum(on_diffs * diffs[:, at] + on_steps * steps[:, at], axis=0, keepdims=True))
         at = pl.ds(pl.multiple_of(number * 8, 8), 8)
         out_ref[at, :] = scale * gradient_ref[at, :] + jnp.concatenate(rows, axis=0)
         return 0
@@ -295,21 +416,24 @@
     lax.fori_loop(0, out_ref.shape[0] // 8, body, 0, unroll=2)
 
 
-def directions(grams, products, gradient, steps, diffs):
+def directions(total, products, gradient, steps, diffs):
     mem, width = steps.shape
-    chunk = min(width, 16384)
-    whole = pl.BlockSpec((mem, LANES), lambda i: (0, 0))
-    flat = pl.BlockSpec((chunk // LANES, LANES), lambda i: (i, 0))
-    wide = pl.BlockSpec((mem, chunk), lambda i: (0, i))
     return pl.pallas_call(
         direction_kernel,
-        grid=(width // chunk,),
-        in_specs=[whole, whole, flat, wide, wide],
-        out_specs=flat,
+        in_specs=[VMEM] * 3 + [HBM] * 2,
+        out_specs=VMEM,
         out_shape=jax.ShapeDtypeStruct(gradient.shape, F32),
-        scratch_shapes=[pltpu.VMEM((3, mem, LANES), F32)],
+        scratch_shapes=[
+            pltpu.VMEM((mem, width), F32),
+            pltpu.VMEM((mem, width), F32),
+            pltpu.SemaphoreType.DMA((2,)),
+        ]
+        + sum_scratch((mem, LANES)),
+        compiler_params=pltpu.CompilerParams(
+            vmem_limit_bytes=40 << 20, collective_id=2, has_side_effects=True
+        ),
         name="direction",
-    )(grams, products, gradient, steps, diffs)
+    )(total, products, gradient, steps, diffs)
 
 
 def local(feature_high, feature_low, labels, weights, history_steps, history_diffs):
@@ -319,19 +443,14 @@
     bits = width.bit_length() - 1
     slots = feature_high.shape[0]
     subs = parts * feature_high.shape[1] // 1024
-    mine = jnp.concatenate([feature_high, feature_low, labels[None, :]], axis=0)
-    every = lax.all_gather(mine, "dp", axis=1)
-    high, low = every[:slots], every[slots : 2 * slots]
-    label = every[2 * slots].reshape(parts // 8, 8, 2, LANES).transpose(1, 0, 2, 3).reshape(8, subs, LANES)
     table = weights.reshape(width // LANES, LANES)
-    partial_gram = gram(history_steps, history_diffs)
-    margin, listed, levels = margins(high, low, table, count, subs, bits)
-    margin, grams = lax.psum((margin, partial_gram), ("dp", "table"))
+    every, partial_gram = share(feature_high, feature_low, labels, history_steps, history_diffs)
+    margin, listed, levels = margins(every, table, count, subs, bits, slots)
+    total = reduced(margin, partial_gram)
     gradient, products = gradients(
-        margin, label, listed, levels, table, history_steps, history_diffs, subs, bits
+        total, every, listed, levels, table, history_steps, history_diffs, subs, bits, 2 * slots
     )
-    products = lax.psum(products, ("dp", "table"))
-    return directions(grams, products, gradient, history_steps, history_diffs).reshape(-1)
+    return directions(total, products, gradient, history_steps, history_diffs).reshape(-1)
 
 
 def solution(mesh):

time: 170 us -> 88.5 us (0.52)
  blocking collectives: 113 us -> 0 us
  Pallas kernels: 50.4 us -> 75.4 us
  local copies, waits for them, and re-layouts: 5.37 us -> 13 us
    psum x2 -> x0, blocking collectives: 80.6 us -> none  [local(): margin, grams = lax.psum((margin, partial_gram), ('dp', 'table'))]
    all_gather x1 -> x0, blocking collectives: 32.8 us -> none  [local(): every = lax.all_gather(mine, 'dp', axis=1)]
    pallas_call x4 -> x5, Pallas kernels: 50.4 us -> 75.4 us  [the longest x1 17.8 us: reduced(): pl.pallas_call(reduce_kernel, in_specs=[VMEM] * 2, out_specs=VMEM, out_sh...]
    unnamed x18 -> x23, local copies, waits for them, and re-layouts: 5.31 us -> 13 us
where the time goes in v2:
time: 88.5 us
  Pallas kernels  75.4 us (85%)
  local copies, waits for them, and re-layouts  13 us (15%)
    pallas_call x1, Pallas kernels, reduced(): pl.pallas_call(reduce_kernel, in_specs=[VMEM] * 2, out_specs=VMEM, out_sh...  17.8 us
    pallas_call x1, Pallas kernels, gradients(): pl.pallas_call(functools.partial(gradient_kernel, subs, bits, label_row),...  15.9 us
    pallas_call x1, Pallas kernels, directions(): pl.pallas_call(direction_kernel, in_specs=[VMEM] * 3 + [HBM] * 2, out_spe...  14.4 us
    pallas_call x1, Pallas kernels, margins(): pl.pallas_call(functools.partial(margin_kernel, count, subs, bits, slots)...  14.1 us
    pallas_call x1, Pallas kernels, share(): pl.pallas_call(share_kernel, in_specs=[VMEM] * 3 + [HBM] * 2, out_specs=[...  13.2 us
    unnamed x23, local copies, waits for them, and re-layouts  13 us

profile of v2, /device:TPU:0, one launch (start us, length us, event | category | flops | bytes accessed | tf_op | source)
XLA Modules:
  0.0 88.5 jit_solution(9413796016398050618)
XLA Ops:
  0.0 0.0 copy-start
  0.0 2.2 %copy-done = f32[8,131072]{1,0:T(8,128)S(1)} copy-done((f32[8,131072]{1,0:T(8,128)S(1)}, f32[8,131072]{1,0:T(8,128)}, u32[]{:S(2)}) %copy-start) | copy-done | bytes 4194328
  2.2 0.0 copy-start.2
  2.2 2.2 %copy-done.2 = f32[8,131072]{1,0:T(8,128)S(1)} copy-done((f32[8,131072]{1,0:T(8,128)S(1)}, f32[8,131072]{1,0:T(8,128)}, u32[]{:S(2)}) %copy-start.2) | copy-done | bytes 4194328
  4.4 0.0 copy-start.6
  4.4 0.7 copy-done.6
  5.1 0.0 copy-start.7
  5.1 0.7 copy-done.7
  5.9 0.0 copy-start.10
  5.9 0.7 copy-done.10
  6.5 0.0 copy-start.4
  6.5 13.2 %share.1 = (s32[8,48,256]{2,1,0:T(8,128)S(1)}, f32[8,128]{1,0:T(8,128)S(1)}) custom-call(s32[20,256]{1,0:T(8,128)S(1)} %copy-done.6, s32[20,256]{1,0:T(8,128)S(1)} %copy-done.7, s32[1,256]{1,0:T(1,128)S(1)} %bitcast.6, f32[8,131072]{1,0:T(8,128)S(1)} %copy-done, f32[8,131072]{1,0:T(8,128)S(1)} %copy-done.2), custom_call_target="tpu_custom_call" | custom-call | tf_op jit(solution)/shard_map/share/pallas_call | solution.py:149
  19.7 0.0 copy-start.9
  19.7 0.0 copy-done.4
  19.8 14.1 %margins.1 = (f32[2,8,128]{2,1,0:T(8,128)S(1)}, s32[8,160,128]{2,1,0:T(8,128)S(1)}, s32[8]{0:T(128)S(1)}) custom-call(s32[8,48,256]{2,1,0:T(8,128)S(1)} %get-tuple-element.12.every_ref, f32[1024,128]{1,0:T(8,128)S(1)} %bitcast.4), custom_call_target="tpu_custom_call" | custom-call | tf_op jit(solution)/shard_map/margins/pallas_call | solution.py:260
  33.8 0.0 copy-done.9
  33.8 0.0 copy-start.8
  33.8 0.6 copy-done.8
  34.4 17.8 %reduce.1.total_ref = f32[3,8,128]{2,1,0:T(8,128)} custom-call(f32[2,8,128]{2,1,0:T(8,128)} %copy-done.8, f32[8,128]{1,0:T(8,128)} %copy-done.9), custom_call_target="tpu_custom_call" | custom-call | tf_op jit(solution)/shard_map/reduce/pallas_call | solution.py:182
  52.3 0.0 copy-start.1
  52.3 2.2 %copy-done.1 = f32[8,131072]{1,0:T(8,128)S(1)} copy-done((f32[8,131072]{1,0:T(8,128)S(1)}, f32[8,131072]{1,0:T(8,128)}, u32[]{:S(2)}) %copy-start.1) | copy-done | bytes 4194328
  54.5 0.0 copy-start.3
  54.5 2.2 %copy-done.3 = f32[8,131072]{1,0:T(8,128)S(1)} copy-done((f32[8,131072]{1,0:T(8,128)S(1)}, f32[8,131072]{1,0:T(8,128)}, u32[]{:S(2)}) %copy-start.3) | copy-done | bytes 4194328
  56.6 0.0 copy-start.5
  56.6 0.7 copy-done.5
  57.4 15.9 %gradient.1 = (f32[1024,128]{1,0:T(8,128)S(1)}, f32[8,128]{1,0:T(8,128)S(1)}) custom-call(f32[3,8,128]{2,1,0:T(8,128)S(1)} %copy-done.5, s32[8,48,256]{2,1,0:T(8,128)S(1)} %get-tuple-element.12.every_ref, s32[8,160,128]{2,1,0:T(8,128)S(1)} %get-tuple-element.15.slots_ref, s32[8]{0:T(128)S(1)} %get-tuple-element.16.levels_ref, f32[1024,128]{1,0:T(8,128)S(1)} %bitcast.5, ...), custom_call_target="tpu_custom_call" | custom-call | tf_op jit(solution)/shard_map/gradient/pallas_call | solution.py:341
  73.3 14.4 %direction.1 = f32[1024,128]{1,0:T(8,128)S(1)} custom-call(f32[3,8,128]{2,1,0:T(8,128)S(1)} %copy-done.5, f32[8,128]{1,0:T(8,128)S(1)} %get-tuple-element.17.products_ref, f32[1024,128]{1,0:T(8,128)S(1)} %get-tuple-element.18.gradient_ref, f32[8,131072]{1,0:T(8,128)S(1)} %copy-done.1, f32[8,131072]{1,0:T(8,128)S(1)} %copy-done.3), custom_call_target="tpu_custom_call" | custom-call | tf_op jit(solution)/shard_map/direction/pallas_call | solution.py:421
  87.7 0.8 copy.8
Async XLA Ops:
  0.0 2.2 %copy-start = (f32[8,131072]{1,0:T(8,128)S(1)}, f32[8,131072]{1,0:T(8,128)}, u32[]{:S(2)}) copy-start(f32[8,131072]{1,0:T(8,128)} %steps_hbm.5) | copy-start | bytes 12582916
  2.2 2.2 %copy-start.2 = (f32[8,131072]{1,0:T(8,128)S(1)}, f32[8,131072]{1,0:T(8,128)}, u32[]{:S(2)}) copy-start(f32[8,131072]{1,0:T(8,128)} %diffs_hbm.5) | copy-start | bytes 12582916
  4.4 0.7 copy-start.6
  5.1 0.7 copy-start.7
  5.9 0.7 copy-start.10
  6.5 13.2 %copy-start.4 = (f32[131072]{0:T(1024)S(1)}, f32[131072]{0:T(1024)}, u32[]{:S(2)}) copy-start(f32[131072]{0:T(1024)} %param.9) | copy-start | bytes 1572868
  19.7 14.1 %copy-start.9 = (f32[8,128]{1,0:T(8,128)}, f32[8,128]{1,0:T(8,128)S(1)}, u32[]{:S(2)}) copy-start(f32[8,128]{1,0:T(8,128)S(1)} %get-tuple-element.14.gram_ref) | copy-start | bytes 12292
  33.8 0.6 copy-start.8
  52.3 2.2 %copy-start.1 = (f32[8,131072]{1,0:T(8,128)S(1)}, f32[8,131072]{1,0:T(8,128)}, u32[]{:S(2)}) copy-start(f32[8,131072]{1,0:T(8,128)} %steps_hbm.5) | copy-start | bytes 12582916
  54.5 2.2 %copy-start.3 = (f32[8,131072]{1,0:T(8,128)S(1)}, f32[8,131072]{1,0:T(8,128)}, u32[]{:S(2)}) copy-start(f32[8,131072]{1,0:T(8,128)} %diffs_hbm.5) | copy-start | bytes 12582916
  56.6 0.7 copy-start.5

commit v3 on v2

--- a/solution.py
+++ b/solution.py
@@ -17,6 +17,7 @@
 slot_mult = (1543, 3079, 769, 3457)
 shifts = (0, 1048573, 2097143, 3145727)
 l2_weight = 1.0
+BUDGET = 60 << 20
 F32, BF16, I32 = jnp.float32, jnp.bfloat16, jnp.int32
 MESH = pl.DeviceIdType.MESH
 VMEM = pl.BlockSpec(memory_space=pltpu.VMEM)
@@ -66,16 +67,18 @@
     return copies
 
 
-def all_sum(mine, near, far, near_sems, far_sems):
-    total = mine
-    for axis, held, sems in (("table", near, near_sems), ("dp", far, far_sems)):
-        me = lax.axis_index(axis)
-        held[me] = total
-        for copy in send(held.at[me], held.at[me], others(axis), *sems):
-            copy.wait()
-        total = held[0]
-        for number in range(1, held.shape[0]):
-            total = total + held[number]
+def stage(axis, held, value, sems):
+    me = lax.axis_index(axis)
+    held[me] = value
+    return send(held.at[me], held.at[me], others(axis), *sems)
+
+
+def finish(copies, held):
+    for copy in copies:
+        copy.wait()
+    total = held[0]
+    for number in range(1, held.shape[0]):
+        total = total + held[number]
     return total
 
 
@@ -91,18 +94,68 @@
     ]
 
 
+def load(steps_hbm, diffs_hbm, steps, diffs, sems, first=0):
+    parts, width = sems.shape[1], steps.shape[1]
+    pairs = []
+    for part in range(parts):
+        size = width // parts
+        pair = []
+        for kind, (source, target) in enumerate(((steps_hbm, steps), (diffs_hbm, diffs))):
+            copy = pltpu.make_async_copy(
+                source.at[:, pl.ds(first + part * size, size)],
+                target.at[:, pl.ds(part * size, size)],
+                sems.at[kind, part],
+            )
+            copy.start()
+            pair.append(copy)
+        pairs.append(pair)
+    return pairs
+
+
+def gram_part(steps, diffs, pairs, part, carry):
+    mem = steps.shape[0]
+    each = steps.shape[1] // len(pairs) // LANES
+    for copy in pairs[part]:
+        copy.wait()
+
+    def body(number, carry):
+        at = pl.ds(pl.multiple_of(number * LANES, LANES), LANES)
+        step, diff = steps[:, at], diffs[:, at]
+        new = []
+        for i in range(mem):
+            row = jnp.broadcast_to(diffs[i : i + 1, at], diff.shape)
+            new.append(carry[2 * i] + step * row)
+            new.append(carry[2 * i + 1] + diff * row)
+        return tuple(new)
+
+    return lax.fori_loop(part * each, (part + 1) * each, body, carry, unroll=4)
+
+
+def to_row(columns):
+    mem = columns[0].shape[0]
+    total = jnp.zeros((mem, LANES), F32)
+    spot = iota((mem, LANES), 1) - iota((mem, LANES), 0)
+    for number, column in enumerate(columns):
+        total = jnp.where(spot == number * mem, jnp.sum(column, axis=1, keepdims=True), total)
+    return jnp.sum(total, axis=0, keepdims=True)
+
+
+def from_row(row, number, mem):
+    spot = iota((mem, LANES), 1) - iota((mem, LANES), 0)
+    wide = jnp.broadcast_to(row, (mem, LANES))
+    column = jnp.sum(jnp.where(spot == number * mem, wide, 0.0), axis=1, keepdims=True)
+    return jnp.broadcast_to(column, (mem, LANES))
+
+
+def gram_row(carry, mem):
+    return to_row([carry[2 * i] for i in range(mem)] + [carry[2 * i + 1] for i in range(mem)])
+
+
 def share_kernel(high_ref, low_ref, labels_ref, steps_hbm, diffs_hbm, every_ref, gram_ref,
-                 steps, diffs, send_sems, recv_sems, step_sems, diff_sems):
-    mem, width = steps.shape
+                 steps, diffs, send_sems, recv_sems, sems):
+    mem = steps.shape[0]
     slots = high_ref.shape[0]
-    parts = step_sems.shape[0]
-    copies = []
-    for part in range(parts):
-        at = (slice(None), pl.ds(part * (width // parts), width // parts))
-        for source, target, sems in ((steps_hbm, steps, step_sems), (diffs_hbm, diffs, diff_sems)):
-            copy = pltpu.make_async_copy(source.at[at], target.at[at], sems.at[part])
-            copy.start()
-            copies.append(copy)
+    pairs = load(steps_hbm, diffs_hbm, steps, diffs, sems)
     me = lax.axis_index("dp")
     every_ref[me, :slots] = high_ref[...]
     every_ref[me, slots : 2 * slots] = low_ref[...]
@@ -113,30 +166,10 @@
     peers = others("dp")
     greet(peers)
     sent = send(every_ref.at[me], every_ref.at[me], peers, send_sems, recv_sems)
-
-    def body(number, carry):
-        at = pl.ds(pl.multiple_of(number * LANES, LANES), LANES)
-        step, diff = steps[:, at], diffs[:, at]
-        new = []
-        for i in range(mem):
-            row = jnp.broadcast_to(diff[i : i + 1], diff.shape)
-            new.append(carry[2 * i] + step * row)
-            new.append(carry[2 * i + 1] + diff * row)
-        return tuple(new)
-
-    final = (jnp.zeros((mem, LANES), F32),) * (2 * mem)
-    each = width // parts // LANES
-    for part in range(parts):
-        copies[2 * part].wait()
-        copies[2 * part + 1].wait()
-        final = lax.fori_loop(part * each, (part + 1) * each, body, final, unroll=4)
-    lane = iota((mem, LANES), 1)
-    total = jnp.zeros((mem, LANES), F32)
-    for i in range(mem):
-        for kind in range(2):
-            column = jnp.sum(final[2 * i + kind], axis=1, keepdims=True)
-            total = jnp.where(lane == kind * mem + i, column, total)
-    gram_ref[...] = total
+    carry = (jnp.zeros((mem, LANES), F32),) * (2 * mem)
+    for part in range(len(pairs)):
+        carry = gram_part(steps, diffs, pairs, part, carry)
+    gram_ref[...] = gram_row(carry, mem)
     for copy in sent:
         copy.wait()
 
@@ -145,49 +178,63 @@
     mem, width = steps.shape
     rows = -(-(2 * high.shape[0] + 1) // 8) * 8
     dp = lax.axis_size("dp")
-    parts = 4
     return pl.pallas_call(
         share_kernel,
         in_specs=[VMEM] * 3 + [HBM] * 2,
         out_specs=[VMEM] * 2,
         out_shape=[
             jax.ShapeDtypeStruct((dp, rows, high.shape[1]), I32),
-            jax.ShapeDtypeStruct((mem, LANES), F32),
+            jax.ShapeDtypeStruct((1, LANES), F32),
         ],
         scratch_shapes=[
-            pltpu.VMEM((mem, width), F32),
-            pltpu.VMEM((mem, width), F32),
+            pltpu.VMEM((mem, width // 2), F32),
+            pltpu.VMEM((mem, width // 2), F32),
             pltpu.SemaphoreType.DMA((dp - 1,)),
             pltpu.SemaphoreType.DMA((dp - 1,)),
-            pltpu.SemaphoreType.DMA((parts,)),
-            pltpu.SemaphoreType.DMA((parts,)),
+            pltpu.SemaphoreType.DMA((2, 2)),
         ],
         compiler_params=pltpu.CompilerParams(
-            vmem_limit_bytes=40 << 20, collective_id=0, has_side_effects=True
+            vmem_limit_bytes=BUDGET, collective_id=0, has_side_effects=True
         ),
         name="share",
     )(high, low, labels.reshape(1, -1), steps, diffs)
 
 
-def reduce_kernel(margin_ref, gram_ref, out_ref, own, near, far, *sems):
-    subs = margin_ref.shape[0]
+def reduce_kernel(margin_ref, gram_ref, steps_hbm, diffs_hbm, out_ref, grams_ref,
+                  steps, diffs, load_sems, near, far, *sems):
+    mem, half = steps.shape
+    pairs = load(steps_hbm, diffs_hbm, steps, diffs, load_sems, half)
     greet(others("table") + others("dp"))
-    own[:subs] = margin_ref[...]
-    own[subs] = gram_ref[...]
-    out_ref[...] = all_sum(own[...], near, far, sems[:2], sems[2:])
-
-
-def reduced(margin, grams):
-    shape = (margin.shape[0] + 1, *margin.shape[1:])
+    carry = (jnp.zeros((mem, LANES), F32),) * (2 * mem)
+    copies = stage("table", near, margin_ref[...], sems[:2])
+    carry = gram_part(steps, diffs, pairs, 0, carry)
+    copies = stage("dp", far, finish(copies, near), sems[2:])
+    carry = gram_part(steps, diffs, pairs, 1, carry)
+    grams_ref[...] = gram_ref[...] + gram_row(carry, mem)
+    out_ref[...] = finish(copies, far)
+
+
+def reduced(margin, grams, steps, diffs):
+    mem, width = steps.shape
     return pl.pallas_call(
         reduce_kernel,
-        in_specs=[VMEM] * 2,
-        out_specs=VMEM,
-        out_shape=jax.ShapeDtypeStruct(shape, F32),
-        scratch_shapes=[pltpu.VMEM(shape, F32)] + sum_scratch(shape),
-        compiler_params=pltpu.CompilerParams(collective_id=1, has_side_effects=True),
+        in_specs=[VMEM] * 2 + [HBM] * 2,
+        out_specs=[VMEM] * 2,
+        out_shape=[
+            jax.ShapeDtypeStruct(margin.shape, F32),
+            jax.ShapeDtypeStruct((1, LANES), F32),
+        ],
+        scratch_shapes=[
+            pltpu.VMEM((mem, width // 2), F32),
+            pltpu.VMEM((mem, width // 2), F32),
+            pltpu.SemaphoreType.DMA((2, 2)),
+        ]
+        + sum_scratch(margin.shape),
+        compiler_params=pltpu.CompilerParams(
+            vmem_limit_bytes=BUDGET, collective_id=1, has_side_effects=True
+        ),
         name="reduce",
-    )(margin, grams)
+    )(margin, grams, steps, diffs)
 
 
 def margin_kernel(count, subs, bits, slot_total, every_ref, weights_ref, margin_ref, slots_ref, levels_ref, table, features):
@@ -270,19 +317,13 @@
             pltpu.VMEM((2 * LANES, (1 << bits) // LANES), BF16),
             pltpu.VMEM((2 * slots, every.shape[0], every.shape[2]), I32),
         ],
-        compiler_params=pltpu.CompilerParams(vmem_limit_bytes=40 << 20),
+        compiler_params=pltpu.CompilerParams(vmem_limit_bytes=BUDGET),
         name="margins",
     )(every, weights)
 
 
-def gradient_kernel(subs, bits, label_row, total_ref, every_ref, slots_ref, levels_ref, weights_ref, steps_hbm, diffs_hbm,
-                    gradient_ref, products_ref, residual, both, steps, diffs, sems):
-    copies = [
-        pltpu.make_async_copy(steps_hbm, steps, sems.at[0]),
-        pltpu.make_async_copy(diffs_hbm, diffs, sems.at[1]),
-    ]
-    for copy in copies:
-        copy.start()
+def gradient_kernel(subs, bits, label_row, total_ref, every_ref, slots_ref, levels_ref, weights_ref,
+                    gradient_ref, residual, both):
     width = 1 << bits
     for sub in range(subs):
         label = every_ref[sub // 2 * 8 : sub // 2 * 8 + 8, label_row, sub % 2 * LANES : sub % 2 * LANES + LANES]
@@ -312,65 +353,34 @@
 
     lax.fori_loop(0, 8, rows, 0)
     gradient_ref[...] = both[:, :LANES] + both[:, LANES:] + l2_weight * weights_ref[...]
-    for copy in copies:
-        copy.wait()
-    mem = steps.shape[0]
-
-    def body(number, carry):
-        by_step, by_diff = carry
-        tile = gradient_ref[pl.ds(pl.multiple_of(number * 8, 8), 8), :]
-        for i in range(8):
-            at = pl.ds(pl.multiple_of(number * 8 * LANES, LANES) + i * LANES, LANES)
-            row = jnp.broadcast_to(tile[i : i + 1], (mem, LANES))
-            by_step = by_step + steps[:, at] * row
-            by_diff = by_diff + diffs[:, at] * row
-        return by_step, by_diff
-
-    zero = jnp.zeros((mem, LANES), F32)
-    by_step, by_diff = lax.fori_loop(0, width // (8 * LANES), body, (zero, zero))
-    lane = iota((mem, LANES), 1)
-    products_ref[...] = jnp.where(
-        lane == 0,
-        jnp.sum(by_step, axis=1, keepdims=True),
-        jnp.where(lane == 1, jnp.sum(by_diff, axis=1, keepdims=True), 0.0),
-    )
-
-
-def gradients(total, every, slots, levels, weights, steps, diffs, subs, bits, label_row):
-    mem, width = steps.shape
+
+
+def gradients(total, every, slots, levels, weights, subs, bits, label_row):
     return pl.pallas_call(
         functools.partial(gradient_kernel, subs, bits, label_row),
-        in_specs=[VMEM, VMEM, VMEM, SMEM, VMEM, HBM, HBM],
-        out_specs=[VMEM, VMEM],
-        out_shape=[jax.ShapeDtypeStruct(weights.shape, F32), jax.ShapeDtypeStruct((mem, LANES), F32)],
+        in_specs=[VMEM, VMEM, VMEM, SMEM, VMEM],
+        out_specs=VMEM,
+        out_shape=jax.ShapeDtypeStruct(weights.shape, F32),
         scratch_shapes=[
             pltpu.VMEM((8, subs, LANES), F32),
-            pltpu.VMEM((width // LANES, 2 * LANES), F32),
-            pltpu.VMEM((mem, width), F32),
-            pltpu.VMEM((mem, width), F32),
-            pltpu.SemaphoreType.DMA((2,)),
-        ],
-        compiler_params=pltpu.CompilerParams(vmem_limit_bytes=40 << 20),
+            pltpu.VMEM((weights.shape[0], 2 * LANES), F32),
+        ],
+        compiler_params=pltpu.CompilerParams(vmem_limit_bytes=BUDGET),
         name="gradient",
-    )(total, every, slots, levels, weights, steps, diffs)
+    )(total, every, slots, levels, weights)
 
 
 def coefficients(grams, products, mem):
-    lane, place = iota((mem, LANES), 1), iota((mem, LANES), 0)
-
-    def column(array, number):
-        return jnp.broadcast_to(
-            jnp.sum(jnp.where(lane == number, array, 0.0), axis=1, keepdims=True), (mem, LANES)
-        )
+    place = iota((mem, LANES), 0)
 
     def pick(array, number):
         return jnp.broadcast_to(array[number : number + 1], (mem, LANES))
 
-    cross = [column(grams, i) for i in range(mem)]
-    square = [column(grams, mem + i) for i in range(mem)]
+    cross = [from_row(grams, i, mem) for i in range(mem)]
+    square = [from_row(grams, mem + i, mem) for i in range(mem)]
     pairs = [pick(cross[i], i) for i in range(mem)]
     inverse = [1.0 / pair for pair in pairs]
-    by_step, by_diff = column(products, 0), column(products, 1)
+    by_step, by_diff = from_row(products, 0, mem), from_row(products, 1, mem)
     alphas = [None] * mem
     for i in reversed(range(mem)):
         alphas[i] = inverse[i] * pick(by_step, i)
@@ -388,21 +398,44 @@
     return scale, on_diffs, on_steps
 
 
-def direction_kernel(total_ref, products_ref, gradient_ref, steps_hbm, diffs_hbm, out_ref,
-                     steps, diffs, local_sems, near, far, *sems):
-    mem = steps.shape[0]
-    copies = [
-        pltpu.make_async_copy(steps_hbm, steps, local_sems.at[0]),
-        pltpu.make_async_copy(diffs_hbm, diffs, local_sems.at[1]),
+def direction_kernel(grams_ref, gradient_ref, steps_hbm, diffs_hbm, out_ref,
+                     steps, diffs, load_sems, held, send_sems, recv_sems):
+    mem, width = steps.shape
+    pairs = load(steps_hbm, diffs_hbm, steps, diffs, load_sems)
+    near, far = lax.axis_size("table"), lax.axis_size("dp")
+    column, row = lax.axis_index("table"), lax.axis_index("dp")
+    peers = [
+        {"dp": lax.rem(row + down, far), "table": lax.rem(column + across, near)}
+        for down in range(far)
+        for across in range(near)
+        if down or across
     ]
-    for copy in copies:
-        copy.start()
-    greet(others("table") + others("dp"))
-    products = all_sum(products_ref[...], near, far, sems[:2], sems[2:])
-    scale, on_diffs, on_steps = coefficients(total_ref[total_ref.shape[0] - 1], products, mem)
+    barrier = pltpu.get_barrier_semaphore()
+    for peer in peers:
+        pl.semaphore_signal(barrier, inc=1, device_id=peer, device_id_type=MESH)
+
+    def product(number, carry):
+        by_step, by_diff = carry
+        for i in range(8):
+            at = pl.ds(pl.multiple_of(number * 8 * LANES, LANES) + i * LANES, LANES)
+            line = jnp.broadcast_to(gradient_ref[pl.ds(number * 8 + i, 1), :], (mem, LANES))
+            by_step = by_step + steps[:, at] * line
+            by_diff = by_diff + diffs[:, at] * line
+        return by_step, by_diff
+
+    carry = (jnp.zeros((mem, LANES), F32),) * 2
+    each = width // len(pairs) // (8 * LANES)
+    for part, pair in enumerate(pairs):
+        for copy in pair:
+            copy.wait()
+        carry = lax.fori_loop(part * each, (part + 1) * each, product, carry)
+    me = row * near + column
+    held[me, 0:1] = grams_ref[...]
+    held[me, 1:2] = to_row(carry)
+    pl.semaphore_wait(barrier, len(peers))
+    total = finish(send(held.at[me], held.at[me], peers, send_sems, recv_sems), held)
+    scale, on_diffs, on_steps = coefficients(total[0:1], total[1:2], mem)
     scale, on_diffs, on_steps = -scale, -on_diffs, -on_steps
-    for copy in copies:
-        copy.wait()
 
     def body(number, _):
         rows = []
@@ -416,24 +449,27 @@
     lax.fori_loop(0, out_ref.shape[0] // 8, body, 0, unroll=2)
 
 
-def directions(total, products, gradient, steps, diffs):
+def directions(grams, gradient, steps, diffs):
     mem, width = steps.shape
+    devices = lax.axis_size("dp") * lax.axis_size("table")
     return pl.pallas_call(
         direction_kernel,
-        in_specs=[VMEM] * 3 + [HBM] * 2,
+        in_specs=[VMEM] * 2 + [HBM] * 2,
         out_specs=VMEM,
         out_shape=jax.ShapeDtypeStruct(gradient.shape, F32),
         scratch_shapes=[
             pltpu.VMEM((mem, width), F32),
             pltpu.VMEM((mem, width), F32),
-            pltpu.SemaphoreType.DMA((2,)),
-        ]
-        + sum_scratch((mem, LANES)),
+            pltpu.SemaphoreType.DMA((2, 4)),
+            pltpu.VMEM((devices, 2, LANES), F32),
+            pltpu.SemaphoreType.DMA((devices - 1,)),
+            pltpu.SemaphoreType.DMA((devices - 1,)),
+        ],
         compiler_params=pltpu.CompilerParams(
-            vmem_limit_bytes=40 << 20, collective_id=2, has_side_effects=True
+            vmem_limit_bytes=BUDGET, collective_id=2, has_side_effects=True
         ),
         name="direction",
-    )(total, products, gradient, steps, diffs)
+    )(grams, gradient, steps, diffs)
 
 
 def local(feature_high, feature_low, labels, weights, history_steps, history_diffs):
@@ -446,11 +482,9 @@
     table = weights.reshape(width // LANES, LANES)
     every, partial_gram = share(feature_high, feature_low, labels, history_steps, history_diffs)
     margin, listed, levels = margins(every, table, count, subs, bits, slots)
-    total = reduced(margin, partial_gram)
-    gradient, products = gradients(
-        total, every, listed, levels, table, history_steps, history_diffs, subs, bits, 2 * slots
-    )
-    return directions(total, products, gradient, history_steps, history_diffs).reshape(-1)
+    total, grams = reduced(margin, partial_gram, history_steps, history_diffs)
+    gradient = gradients(total, every, listed, levels, table, subs, bits, 2 * slots)
+    return directions(grams, gradient, history_steps, history_diffs).reshape(-1)
 
 
 def solution(mesh):

time: 88.5 us -> 83.3 us (0.941); the launches traced: 88.5 us -> 81.8 us
  local copies, waits for them, and re-layouts: 13 us -> 1.87 us
  Pallas kernels: 75.4 us -> 79.9 us
    unnamed x23 -> x1, local copies, waits for them, and re-layouts: 13 us -> 1.87 us
    pallas_call x2, Pallas kernels: 32.2 us -> 34.4 us  [the longest x1 17.2 us: reduced(): pl.pallas_call(reduce_kernel, in_specs=[VMEM] * 2 + [HBM] * 2, out_specs=...]
    pallas_call x1, Pallas kernels: 14.1 us -> 15.9 us  [margins(): pl.pallas_call(functools.partial(margin_kernel, count, subs, bits, slots)...]
    pallas_call x1, Pallas kernels: 13.2 us -> 14.1 us  [share(): pl.pallas_call(share_kernel, in_specs=[VMEM] * 3 + [HBM] * 2, out_specs=[...]
where the time goes in v3:
time: 83.3 us; the launch traced here: 81.8 us
  Pallas kernels  79.9 us (96%)
  local copies, waits for them, and re-layouts  1.87 us (2%)
    pallas_call x1, Pallas kernels, reduced(): pl.pallas_call(reduce_kernel, in_specs=[VMEM] * 2 + [HBM] * 2, out_specs=...  17.2 us
    pallas_call x1, Pallas kernels, directions(): pl.pallas_call(direction_kernel, in_specs=[VMEM] * 2 + [HBM] * 2, out_spe...  17.2 us
    pallas_call x1, Pallas kernels, margins(): pl.pallas_call(functools.partial(margin_kernel, count, subs, bits, slots)...  15.9 us
    pallas_call x1, Pallas kernels, gradients(): pl.pallas_call(functools.partial(gradient_kernel, subs, bits, label_row),...  15.5 us
    pallas_call x1, Pallas kernels, share(): pl.pallas_call(share_kernel, in_specs=[VMEM] * 3 + [HBM] * 2, out_specs=[...  14.1 us
    unnamed x1, local copies, waits for them, and re-layouts  1.87 us

profile of v3, /device:TPU:0, one launch (start us, length us, event | category | flops | bytes accessed | tf_op | source)
XLA Modules:
  0.0 81.8 jit_solution(11326285292145263496)
XLA Ops:
  0.0 14.1 %share.1 = (s32[8,48,256]{2,1,0:T(8,128)}, f32[1,128]{1,0:T(1,128)}) custom-call(s32[20,256]{1,0:T(8,128)} %high_ref.1, s32[20,256]{1,0:T(8,128)} %low_ref.1, s32[1,256]{1,0:T(1,128)} %bitcast.6, f32[8,131072]{1,0:T(8,128)} %steps_hbm.5, f32[8,131072]{1,0:T(8,128)} %diffs_hbm.5), custom_call_target="tpu_custom_call" | custom-call | tf_op jit(solution)/shard_map/share/pallas_call | solution.py:181
  14.1 15.9 %margins.1 = (f32[2,8,128]{2,1,0:T(8,128)}, s32[8,160,128]{2,1,0:T(8,128)}, s32[8]{0:T(128)}) custom-call(s32[8,48,256]{2,1,0:T(8,128)} %get-tuple-element.12.every_ref, f32[1024,128]{1,0:T(8,128)} %bitcast.3), custom_call_target="tpu_custom_call" | custom-call | tf_op jit(solution)/shard_map/margins/pallas_call | solution.py:307
  30.0 17.2 %reduce.1 = (f32[2,8,128]{2,1,0:T(8,128)}, f32[1,128]{1,0:T(1,128)}) custom-call(f32[2,8,128]{2,1,0:T(8,128)} %get-tuple-element.13.margin_ref, f32[1,128]{1,0:T(1,128)} %get-tuple-element.14.gram_ref, f32[8,131072]{1,0:T(8,128)} %steps_hbm.5, f32[8,131072]{1,0:T(8,128)} %diffs_hbm.5), custom_call_target="tpu_custom_call" | custom-call | tf_op jit(solution)/shard_map/reduce/pallas_call | solution.py:219
  47.2 15.5 %gradient.1.gradient_ref = f32[1024,128]{1,0:T(8,128)} custom-call(f32[2,8,128]{2,1,0:T(8,128)} %get-tuple-element.16.total_ref, s32[8,48,256]{2,1,0:T(8,128)} %get-tuple-element.12.every_ref, s32[8,160,128]{2,1,0:T(8,128)} %get-tuple-element.17.slots_ref, s32[8]{0:T(128)} %get-tuple-element.18.levels_ref, f32[1024,128]{1,0:T(8,128)} %bitcast.4), custom_call_target="tpu_custom_call" | custom-call | tf_op jit(solution)/shard_map/gradient/pallas_call | solution.py:359
  62.7 17.2 %direction.1 = f32[1024,128]{1,0:T(8,128)} custom-call(f32[1,128]{1,0:T(1,128)} %get-tuple-element.15.grams_ref, f32[1024,128]{1,0:T(8,128)} %gradient.1.gradient_ref, f32[8,131072]{1,0:T(8,128)} %steps_hbm.5, f32[8,131072]{1,0:T(8,128)} %diffs_hbm.5), custom_call_target="tpu_custom_call" | custom-call | tf_op jit(solution)/shard_map/direction/pallas_call | solution.py:455
  79.9 1.9 %copy.8 = f32[131072]{0:T(1024)} copy(f32[131072]{0:T(1024)} %bitcast.5) | data formatting | bytes 1048576

commit v4 on v3

--- a/solution.py
+++ b/solution.py
@@ -17,7 +17,7 @@
 slot_mult = (1543, 3079, 769, 3457)
 shifts = (0, 1048573, 2097143, 3145727)
 l2_weight = 1.0
-BUDGET = 60 << 20
+BUDGET = 50 << 20
 F32, BF16, I32 = jnp.float32, jnp.bfloat16, jnp.int32
 MESH = pl.DeviceIdType.MESH
 VMEM = pl.BlockSpec(memory_space=pltpu.VMEM)
@@ -187,11 +187,11 @@
             jax.ShapeDtypeStruct((1, LANES), F32),
         ],
         scratch_shapes=[
-            pltpu.VMEM((mem, width // 2), F32),
-            pltpu.VMEM((mem, width // 2), F32),
+            pltpu.VMEM((mem, 3 * width // 4), F32),
+            pltpu.VMEM((mem, 3 * width // 4), F32),
             pltpu.SemaphoreType.DMA((dp - 1,)),
             pltpu.SemaphoreType.DMA((dp - 1,)),
-            pltpu.SemaphoreType.DMA((2, 2)),
+            pltpu.SemaphoreType.DMA((2, 3)),
         ],
         compiler_params=pltpu.CompilerParams(
             vmem_limit_bytes=BUDGET, collective_id=0, has_side_effects=True
@@ -202,14 +202,13 @@
 
 def reduce_kernel(margin_ref, gram_ref, steps_hbm, diffs_hbm, out_ref, grams_ref,
                   steps, diffs, load_sems, near, far, *sems):
-    mem, half = steps.shape
-    pairs = load(steps_hbm, diffs_hbm, steps, diffs, load_sems, half)
+    mem, size = steps.shape
+    pairs = load(steps_hbm, diffs_hbm, steps, diffs, load_sems, steps_hbm.shape[1] - size)
     greet(others("table") + others("dp"))
     carry = (jnp.zeros((mem, LANES), F32),) * (2 * mem)
     copies = stage("table", near, margin_ref[...], sems[:2])
     carry = gram_part(steps, diffs, pairs, 0, carry)
     copies = stage("dp", far, finish(copies, near), sems[2:])
-    carry = gram_part(steps, diffs, pairs, 1, carry)
     grams_ref[...] = gram_ref[...] + gram_row(carry, mem)
     out_ref[...] = finish(copies, far)
 
@@ -225,9 +224,9 @@
             jax.ShapeDtypeStruct((1, LANES), F32),
         ],
         scratch_shapes=[
-            pltpu.VMEM((mem, width // 2), F32),
-            pltpu.VMEM((mem, width // 2), F32),
-            pltpu.SemaphoreType.DMA((2, 2)),
+            pltpu.VMEM((mem, width // 4), F32),
+            pltpu.VMEM((mem, width // 4), F32),
+            pltpu.SemaphoreType.DMA((2, 1)),
         ]
         + sum_scratch(margin.shape),
         compiler_params=pltpu.CompilerParams(
@@ -398,6 +397,19 @@
     return scale, on_diffs, on_steps
 
 
+def row_sums(tiles):
+    place = iota((8, LANES), 0)
+    gap = 1
+    while len(tiles) > 1:
+        low = (place & gap) == 0
+        tiles = [
+            jnp.where(low, a, b) + pltpu.roll(jnp.where(low, b, a), 8 - gap, 0)
+            for a, b in zip(tiles[::2], tiles[1::2])
+        ]
+        gap *= 2
+    return tiles[0]
+
+
 def direction_kernel(grams_ref, gradient_ref, steps_hbm, diffs_hbm, out_ref,
                      steps, diffs, load_sems, held, send_sems, recv_sems):
     mem, width = steps.shape
@@ -441,9 +453,9 @@
         rows = []
         for i in range(8):
             at = pl.ds(pl.multiple_of(number * 8 * LANES, LANES) + i * LANES, LANES)
-            rows.append(jnp.sum(on_diffs * diffs[:, at] + on_steps * steps[:, at], axis=0, keepdims=True))
+            rows.append(on_diffs * diffs[:, at] + on_steps * steps[:, at])
         at = pl.ds(pl.multiple_of(number * 8, 8), 8)
-        out_ref[at, :] = scale * gradient_ref[at, :] + jnp.concatenate(rows, axis=0)
+        out_ref[at, :] = scale * gradient_ref[at, :] + row_sums(rows)
         return 0
 
     lax.fori_loop(0, out_ref.shape[0] // 8, body, 0, unroll=2)

time: 83.3 us -> 74.4 us (0.89)
  Pallas kernels: 79.9 us -> 70.6 us
  local copies, waits for them, and re-layouts: 1.87 us -> 2.98 us
    pallas_call x1, Pallas kernels: 17.2 us -> 14.2 us  [directions(): pl.pallas_call(direction_kernel, in_specs=[VMEM] * 2 + [HBM] * 2, out_spe...]
    pallas_call x1, Pallas kernels: 15.5 us -> 12.8 us  [gradients(): pl.pallas_call(functools.partial(gradient_kernel, subs, bits, label_row),...]
    pallas_call x1, Pallas kernels: 15.9 us -> 13.6 us  [margins(): pl.pallas_call(functools.partial(margin_kernel, count, subs, bits, slots)...]
    pallas_call x1, Pallas kernels: 14.1 us -> 12.6 us  [share(): pl.pallas_call(share_kernel, in_specs=[VMEM] * 3 + [HBM] * 2, out_specs=[...]
    unnamed x1 -> x9, local copies, waits for them, and re-layouts: 1.87 us -> 2.98 us
where the time goes in v4:
time: 74.4 us; the launch traced here: 73.6 us
  Pallas kernels  70.6 us (95%)
  local copies, waits for them, and re-layouts  2.98 us (4%)
    pallas_call x1, Pallas kernels, reduced(): pl.pallas_call(reduce_kernel, in_specs=[VMEM] * 2 + [HBM] * 2, out_specs=...  17.3 us
    pallas_call x1, Pallas kernels, directions(): pl.pallas_call(direction_kernel, in_specs=[VMEM] * 2 + [HBM] * 2, out_spe...  14.2 us
    pallas_call x1, Pallas kernels, margins(): pl.pallas_call(functools.partial(margin_kernel, count, subs, bits, slots)...  13.6 us
    pallas_call x1, Pallas kernels, gradients(): pl.pallas_call(functools.partial(gradient_kernel, subs, bits, label_row),...  12.8 us
    pallas_call x1, Pallas kernels, share(): pl.pallas_call(share_kernel, in_specs=[VMEM] * 3 + [HBM] * 2, out_specs=[...  12.6 us
    unnamed x9, local copies, waits for them, and re-layouts  2.98 us

profile of v4, /device:TPU:0, one launch (start us, length us, event | category | flops | bytes accessed | tf_op | source)
XLA Modules:
  0.0 73.6 jit_solution(4787807039454903775)
XLA Ops:
  0.0 0.0 copy-start.1
  0.0 0.7 copy-done.1
  0.7 0.0 copy-start.2
  0.7 0.7 copy-done.2
  1.5 0.0 copy-start.3
  1.5 0.7 copy-done.3
  2.2 0.0 copy-start
  2.2 12.6 %share.1 = (s32[8,48,256]{2,1,0:T(8,128)S(1)}, f32[1,128]{1,0:T(1,128)S(1)}) custom-call(s32[20,256]{1,0:T(8,128)S(1)} %copy-done.1, s32[20,256]{1,0:T(8,128)S(1)} %copy-done.2, s32[1,256]{1,0:T(1,128)S(1)} %bitcast.6, f32[8,131072]{1,0:T(8,128)} %steps_hbm.5, f32[8,131072]{1,0:T(8,128)} %diffs_hbm.5), custom_call_target="tpu_custom_call" | custom-call | tf_op jit(solution)/shard_map/share/pallas_call | solution.py:181
  14.8 0.0 copy-done
  14.8 13.6 %margins.1 = (f32[2,8,128]{2,1,0:T(8,128)S(1)}, s32[8,160,128]{2,1,0:T(8,128)S(1)}, s32[8]{0:T(128)S(1)}) custom-call(s32[8,48,256]{2,1,0:T(8,128)S(1)} %get-tuple-element.12.every_ref, f32[1024,128]{1,0:T(8,128)S(1)} %bitcast.3), custom_call_target="tpu_custom_call" | custom-call | tf_op jit(solution)/shard_map/margins/pallas_call | solution.py:306
  28.4 17.3 %reduce.1 = (f32[2,8,128]{2,1,0:T(8,128)S(1)}, f32[1,128]{1,0:T(1,128)S(1)}) custom-call(f32[2,8,128]{2,1,0:T(8,128)S(1)} %get-tuple-element.13.margin_ref, f32[1,128]{1,0:T(1,128)S(1)} %get-tuple-element.14.gram_ref, f32[8,131072]{1,0:T(8,128)} %steps_hbm.5, f32[8,131072]{1,0:T(8,128)} %diffs_hbm.5), custom_call_target="tpu_custom_call" | custom-call | tf_op jit(solution)/shard_map/reduce/pallas_call | solution.py:218
  45.7 12.8 %gradient.1.gradient_ref = f32[1024,128]{1,0:T(8,128)S(1)} custom-call(f32[2,8,128]{2,1,0:T(8,128)S(1)} %get-tuple-element.16.total_ref, s32[8,48,256]{2,1,0:T(8,128)S(1)} %get-tuple-element.12.every_ref, s32[8,160,128]{2,1,0:T(8,128)S(1)} %get-tuple-element.17.slots_ref, s32[8]{0:T(128)S(1)} %get-tuple-element.18.levels_ref, f32[1024,128]{1,0:T(8,128)S(1)} %bitcast.4), custom_call_target="tpu_custom_call" | custom-call | tf_op jit(solution)/shard_map/gradient/pallas_call | solution.py:358
  58.5 14.2 %direction.1 = f32[1024,128]{1,0:T(8,128)S(1)} custom-call(f32[1,128]{1,0:T(1,128)S(1)} %get-tuple-element.15.grams_ref, f32[1024,128]{1,0:T(8,128)S(1)} %gradient.1.gradient_ref, f32[8,131072]{1,0:T(8,128)} %steps_hbm.5, f32[8,131072]{1,0:T(8,128)} %diffs_hbm.5), custom_call_target="tpu_custom_call" | custom-call | tf_op jit(solution)/shard_map/direction/pallas_call | solution.py:467
  72.8 0.8 %copy.8 = f32[131072]{0:T(1024)} copy(f32[131072]{0:T(1024)S(1)} %bitcast.5) | data formatting | bytes 1048576
Async XLA Ops:
  0.0 0.7 %copy-start.1 = (s32[20,256]{1,0:T(8,128)S(1)}, s32[20,256]{1,0:T(8,128)}, u32[]{:S(2)}) copy-start(s32[20,256]{1,0:T(8,128)} %high_ref.1) | copy-start | bytes 61444
  0.7 0.7 %copy-start.2 = (s32[20,256]{1,0:T(8,128)S(1)}, s32[20,256]{1,0:T(8,128)}, u32[]{:S(2)}) copy-start(s32[20,256]{1,0:T(8,128)} %low_ref.1) | copy-start | bytes 61444
  1.5 0.7 copy-start.3
  2.2 12.6 %copy-start = (f32[131072]{0:T(1024)S(1)}, f32[131072]{0:T(1024)}, u32[]{:S(2)}) copy-start(f32[131072]{0:T(1024)} %param.9) | copy-start | bytes 1572868

commit v5 on v4

--- a/solution.py
+++ b/solution.py
@@ -151,21 +151,15 @@
     return to_row([carry[2 * i] for i in range(mem)] + [carry[2 * i + 1] for i in range(mem)])
 
 
-def share_kernel(high_ref, low_ref, labels_ref, steps_hbm, diffs_hbm, every_ref, gram_ref,
+def share_kernel(mine_ref, steps_hbm, diffs_hbm, every_ref, gram_ref,
                  steps, diffs, send_sems, recv_sems, sems):
     mem = steps.shape[0]
-    slots = high_ref.shape[0]
     pairs = load(steps_hbm, diffs_hbm, steps, diffs, sems)
     me = lax.axis_index("dp")
-    every_ref[me, :slots] = high_ref[...]
-    every_ref[me, slots : 2 * slots] = low_ref[...]
-    every_ref[me, 2 * slots : 2 * slots + 1] = labels_ref[...]
-    if every_ref.shape[1] > 2 * slots + 1:
-        rest = every_ref.shape[1] - 2 * slots - 1
-        every_ref[me, 2 * slots + 1 :] = jnp.zeros((rest, labels_ref.shape[1]), I32)
+    every_ref[me] = mine_ref[...]
     peers = others("dp")
     greet(peers)
-    sent = send(every_ref.at[me], every_ref.at[me], peers, send_sems, recv_sems)
+    sent = send(mine_ref, every_ref.at[me], peers, send_sems, recv_sems)
     carry = (jnp.zeros((mem, LANES), F32),) * (2 * mem)
     for part in range(len(pairs)):
         carry = gram_part(steps, diffs, pairs, part, carry)
@@ -174,16 +168,15 @@
         copy.wait()
 
 
-def share(high, low, labels, steps, diffs):
+def share(mine, steps, diffs):
     mem, width = steps.shape
-    rows = -(-(2 * high.shape[0] + 1) // 8) * 8
     dp = lax.axis_size("dp")
     return pl.pallas_call(
         share_kernel,
-        in_specs=[VMEM] * 3 + [HBM] * 2,
+        in_specs=[VMEM] + [HBM] * 2,
         out_specs=[VMEM] * 2,
         out_shape=[
-            jax.ShapeDtypeStruct((dp, rows, high.shape[1]), I32),
+            jax.ShapeDtypeStruct((dp, *mine.shape), I32),
             jax.ShapeDtypeStruct((1, LANES), F32),
         ],
         scratch_shapes=[
@@ -197,7 +190,7 @@
             vmem_limit_bytes=BUDGET, collective_id=0, has_side_effects=True
         ),
         name="share",
-    )(high, low, labels.reshape(1, -1), steps, diffs)
+    )(mine, steps, diffs)
 
 
 def reduce_kernel(margin_ref, gram_ref, steps_hbm, diffs_hbm, out_ref, grams_ref,
@@ -207,8 +200,8 @@
     greet(others("table") + others("dp"))
     carry = (jnp.zeros((mem, LANES), F32),) * (2 * mem)
     copies = stage("table", near, margin_ref[...], sems[:2])
+    copies = stage("dp", far, finish(copies, near), sems[2:])
     carry = gram_part(steps, diffs, pairs, 0, carry)
-    copies = stage("dp", far, finish(copies, near), sems[2:])
     grams_ref[...] = gram_ref[...] + gram_row(carry, mem)
     out_ref[...] = finish(copies, far)
 
@@ -492,7 +485,8 @@
     slots = feature_high.shape[0]
     subs = parts * feature_high.shape[1] // 1024
     table = weights.reshape(width // LANES, LANES)
-    every, partial_gram = share(feature_high, feature_low, labels, history_steps, history_diffs)
+    mine = jnp.concatenate([feature_high, feature_low, labels[None, :]], axis=0)
+    every, partial_gram = share(mine, history_steps, history_diffs)
     margin, listed, levels = margins(every, table, count, subs, bits, slots)
     total, grams = reduced(margin, partial_gram, history_steps, history_diffs)
     gradient = gradients(total, every, listed, levels, table, subs, bits, 2 * slots)

time: 74.4 us -> 71.8 us (0.965)
  local copies, waits for them, and re-layouts: 2.98 us -> 0.83 us
  Pallas kernels: 70.6 us -> 69.1 us
  other arithmetic: 0 us -> 0.78 us
    unnamed x9 -> x3, local copies, waits for them, and re-layouts: 2.98 us -> 0.83 us
    pallas_call x1, Pallas kernels: 17.3 us -> 15.3 us  [reduced(): pl.pallas_call(reduce_kernel, in_specs=[VMEM] * 2 + [HBM] * 2, out_specs=...]
    concatenate x0 -> x1, other arithmetic: none -> 0.78 us  [local(): mine = jnp.concatenate([feature_high, feature_low, labels[None, :]], axis=0)]
where the time goes in v5:
time: 71.8 us; the launch traced here: 70.7 us
  Pallas kernels  69.1 us (96%)
  local copies, waits for them, and re-layouts  0.83 us (1%)
  other arithmetic  0.78 us (1%)
    pallas_call x1, Pallas kernels, reduced(): pl.pallas_call(reduce_kernel, in_specs=[VMEM] * 2 + [HBM] * 2, out_specs=...  15.3 us
    pallas_call x1, Pallas kernels, margins(): pl.pallas_call(functools.partial(margin_kernel, count, subs, bits, slots)...  14.1 us
    pallas_call x1, Pallas kernels, directions(): pl.pallas_call(direction_kernel, in_specs=[VMEM] * 2 + [HBM] * 2, out_spe...  13.8 us
    pallas_call x1, Pallas kernels, gradients(): pl.pallas_call(functools.partial(gradient_kernel, subs, bits, label_row),...  13.3 us
    pallas_call x1, Pallas kernels, share(): pl.pallas_call(share_kernel, in_specs=[VMEM] + [HBM] * 2, out_specs=[VMEM...  12.6 us

profile of v5, /device:TPU:0, one launch (start us, length us, event | category | flops | bytes accessed | tf_op | source)
XLA Modules:
  0.0 70.7 jit_solution(7751053547132179835)
XLA Ops:
  0.0 0.8 %pad_add_fusion.mine_ref = s32[41,256]{1,0:T(8,128)S(1)} fusion(s32[1,256]{1,0:T(1,128)} %bitcast.6, s32[20,256]{1,0:T(8,128)} %param.7, s32[20,256]{1,0:T(8,128)} %param.6), kind=kLoop, calls=%fused_computation | loop fusion | flops 20992 | bytes 83968 | tf_op jit(solution)/shard_map/concatenate | solution.py:488
  0.8 0.0 copy-start
  0.8 12.6 %share.1 = (s32[8,41,256]{2,1,0:T(8,128)S(1)}, f32[1,128]{1,0:T(1,128)S(1)}) custom-call(s32[41,256]{1,0:T(8,128)S(1)} %pad_add_fusion.mine_ref, f32[8,131072]{1,0:T(8,128)} %steps_hbm.5, f32[8,131072]{1,0:T(8,128)} %diffs_hbm.5), custom_call_target="tpu_custom_call" | custom-call | tf_op jit(solution)/shard_map/share/pallas_call | solution.py:174
  13.4 0.0 copy-done
  13.4 14.1 %margins.1 = (f32[2,8,128]{2,1,0:T(8,128)S(1)}, s32[8,160,128]{2,1,0:T(8,128)S(1)}, s32[8]{0:T(128)S(1)}) custom-call(s32[8,41,256]{2,1,0:T(8,128)S(1)} %get-tuple-element.12.every_ref, f32[1024,128]{1,0:T(8,128)S(1)} %bitcast.3), custom_call_target="tpu_custom_call" | custom-call | tf_op jit(solution)/shard_map/margins/pallas_call | solution.py:299
  27.5 15.3 %reduce.1 = (f32[2,8,128]{2,1,0:T(8,128)S(1)}, f32[1,128]{1,0:T(1,128)S(1)}) custom-call(f32[2,8,128]{2,1,0:T(8,128)S(1)} %get-tuple-element.13.margin_ref, f32[1,128]{1,0:T(1,128)S(1)} %get-tuple-element.14.gram_ref, f32[8,131072]{1,0:T(8,128)} %steps_hbm.5, f32[8,131072]{1,0:T(8,128)} %diffs_hbm.5), custom_call_target="tpu_custom_call" | custom-call | tf_op jit(solution)/shard_map/reduce/pallas_call | solution.py:211
  42.8 13.3 %gradient.1.gradient_ref = f32[1024,128]{1,0:T(8,128)S(1)} custom-call(f32[2,8,128]{2,1,0:T(8,128)S(1)} %get-tuple-element.16.total_ref, s32[8,41,256]{2,1,0:T(8,128)S(1)} %get-tuple-element.12.every_ref, s32[8,160,128]{2,1,0:T(8,128)S(1)} %get-tuple-element.17.slots_ref, s32[8]{0:T(128)S(1)} %get-tuple-element.18.levels_ref, f32[1024,128]{1,0:T(8,128)S(1)} %bitcast.4), custom_call_target="tpu_custom_call" | custom-call | tf_op jit(solution)/shard_map/gradient/pallas_call | solution.py:351
  56.1 13.8 %direction.1 = f32[1024,128]{1,0:T(8,128)S(1)} custom-call(f32[1,128]{1,0:T(1,128)S(1)} %get-tuple-element.15.grams_ref, f32[1024,128]{1,0:T(8,128)S(1)} %gradient.1.gradient_ref, f32[8,131072]{1,0:T(8,128)} %steps_hbm.5, f32[8,131072]{1,0:T(8,128)} %diffs_hbm.5), custom_call_target="tpu_custom_call" | custom-call | tf_op jit(solution)/shard_map/direction/pallas_call | solution.py:460
  69.9 0.8 %copy.8 = f32[131072]{0:T(1024)} copy(f32[131072]{0:T(1024)S(1)} %bitcast.5) | data formatting | bytes 1048576
Async XLA Ops:
  0.8 12.7 %copy-start = (f32[131072]{0:T(1024)S(1)}, f32[131072]{0:T(1024)}, u32[]{:S(2)}) copy-start(f32[131072]{0:T(1024)} %param.9) | copy-start | bytes 1572868
